TPU v7x, 256 devices: a whole 4x4x8 slice. The times are simulated.
256 devices in a mesh: pop: 32 (over x_lo, z, core), tp: 8 (over x_hi, y).
Axes of the slice: x: 4 (x_hi: 2, x_lo: 2; x = x_hi * 2 + x_lo), y: 4, z: 8, core: 2. Of those that a mesh axis runs over, the one named last changes fastest.
Arguments:
- hidden: bfloat16 [2048, 5120], P('pop', 'tp'), may hold values from -24 to 24
- norm_gain: float32 [5120], P('tp'), may hold values from 0.25 to 1.75
- right_factors: bfloat16 [5120, 128], P('tp'), may hold values from -0.078125 to 0.078125
- left_factors: bfloat16 [77824, 128], P(('pop', 'tp')), may hold values from -4 to 4
- targets: int32 [2048], replicated, may hold values from 0 to 77823
- master: float32 [77824, 5120], P(('pop', 'tp')), may hold values from -0.2934839 to 0.2934839
Outputs:
- member_loglik: float32 [64], replicated
- new_master: float32 [77824, 5120], P(('pop', 'tp'))
All inputs are finite; a program needn't handle non-finite values.
Results may differ from a plain program's by a relative error of at most 0.0026.
The roundings to bfloat16 on the way count: a program that leaves them out, or rounds other values in their place, can miss the bound.
Values may be sent and summed in bfloat16 or wider, within the bound.
A program may use at most 128 MiB of HBM per device.

v0:
```python
import jax
import jax.numpy as jnp
from jax import lax
from jax.sharding import PartitionSpec as P

D = 5120
RANK = 4
SEQ = 32


NORM_EPS = 1e-06
SIGMA_NOISE = 0.25
LEARN_RATE = 0.5


def contract(left, right):
    return lax.dot_general(
        left, right, (((1,), (1,)), ((), ())), preferred_element_type=jnp.float32
    )


def body(hidden, norm_gain, right_factors, left_factors, targets, master):
    tok_rows = hidden.shape[0]
    half_rows = tok_rows // 2
    fact_cols = right_factors.shape[1]
    voc_rows = master.shape[0]
    pop_index = lax.axis_index("pop")
    values = hidden.astype(jnp.float32)
    squares = lax.psum(jnp.sum(values * values, axis=1), "tp")
    row_scale = lax.rsqrt(squares / D + NORM_EPS)
    normed = (values * row_scale[:, None] * norm_gain[None, :]).astype(jnp.bfloat16)
    pair_cols = lax.dynamic_slice_in_dim(right_factors, pop_index * RANK, RANK, 1)
    partial_proj = jnp.dot(normed, pair_cols, preferred_element_type=jnp.float32)
    projection = lax.psum(partial_proj, "tp")
    member_sign = jnp.where(jnp.arange(tok_rows) < half_rows, SIGMA_NOISE, -SIGMA_NOISE).astype(
        jnp.float32
    )
    scaled = projection * member_sign[:, None]
    own_block = (lax.iota(jnp.int32, fact_cols) // RANK == pop_index).astype(jnp.float32)
    lowrank = (jnp.tile(scaled, (1, fact_cols // RANK)) * own_block[None, :]).astype(jnp.bfloat16)
    head = master.astype(jnp.bfloat16)
    full_rows, full_right = (
        lax.all_gather(normed, "tp", axis=1, tiled=True),
        lax.all_gather(right_factors, "tp", axis=0, tiled=True),
    )
    joined_rows = jnp.concatenate([full_rows, lowrank], axis=1)
    piece = lax.all_gather(joined_rows, "pop", axis=0, tiled=True)
    logits = contract(piece[:, :D], head) + contract(piece[:, D:], left_factors)
    offset = (pop_index * lax.axis_size("tp") + lax.axis_index("tp")) * voc_rows
    row_max = jnp.max(logits, axis=1)
    column_ids = lax.iota(jnp.int32, voc_rows)
    target_logit = jnp.sum(
        jnp.where(offset + column_ids[None, :] == targets[:, None], logits, 0.0), axis=1
    )
    all_max = lax.pmax(row_max, ("pop", "tp"))
    row_sum = jnp.sum(jnp.exp(logits - all_max[:, None]), axis=1)
    all_sum, all_target = lax.psum((row_sum, target_logit), ("pop", "tp"))
    logprob = all_target - all_max - jnp.log(all_sum)
    member_loglik = jnp.mean(logprob.reshape(-1, SEQ), axis=1)
    fitness = member_loglik[0::2] - member_loglik[1::2]
    weight_cols = jnp.repeat(fitness, RANK)
    scaled_left = (left_factors.astype(jnp.float32) * weight_cols[None, :]).astype(jnp.bfloat16)
    update = contract(scaled_left, full_right)
    new_master = master + LEARN_RATE * update
    return (member_loglik, new_master)


def solution(mesh):
    in_specs = (
        P("pop", "tp"),
        P("tp"),
        P("tp", None),
        P(("pop", "tp"), None),
        P(),
        P(("pop", "tp"), None),
    )
    out_specs = (P(), P(("pop", "tp"), None))
    return jax.shard_map(body, mesh=mesh, in_specs=in_specs, out_specs=out_specs, check_vma=False)
```

profile of v0, /device:TPU:1, one launch (start us, length us, event | category | flops | bytes accessed | tf_op | source)
XLA Modules:
  0.0 395.4 jit_solution(13763955117740881840)
XLA Ops:
  7.2 0.0 copy-start
  7.2 0.0 all-gather.3.cloned.1.call-start
  7.3 1.0 fusion.11
  8.3 21.5 %psum.28 = f32[64]{0:T(128)S(1)} all-reduce(f32[64]{0:T(128)S(1)} %fusion.11), channel_id=1, replica_groups=mesh['pop'=32,'tp'=8] {'tp'}, use_global_device_ids=true, to_apply=%region_1.0 | all-reduce | flops 64 | bytes 512 | tf_op jit(solution)/shard_map/psum | solution.py:29
  29.8 1.0 fusion.13
  30.8 29.9 %all_gather.9 = bf16[64,5120]{1,0:T(8,128)(2,1)S(1)} all-gather(bf16[64,640]{1,0:T(8,128)(2,1)S(1)} %fusion.13), channel_id=1, replica_groups=mesh['pop'=32,'tp'=8] {'tp'}, dimensions={1}, use_global_device_ids=true | all-gather | bytes 737280 | tf_op jit(solution)/shard_map/all_gather | solution.py:43
  60.7 1.2 fusion.14
  61.8 15.7 %psum.29 = f32[64,4]{0,1:T(4,128)S(1)} all-reduce(f32[64,4]{0,1:T(4,128)S(1)} %fusion.14), channel_id=1, replica_groups=mesh['pop'=32,'tp'=8] {'tp'}, use_global_device_ids=true, to_apply=%region_2.0 | all-reduce | flops 256 | bytes 2048 | tf_op jit(solution)/shard_map/psum | solution.py:34
  77.6 0.1 multiply_convert_fusion.2
  77.7 0.1 copy.9
  77.8 0.9 pad_maximum_fusion
  78.7 0.0 all-gather.3.cloned.1.call-update
  78.7 0.0 all-gather.5.cloned.1.call-start
  78.7 0.7 all-gather.5.cloned.1.call-update
  79.5 135.6 %all-gather.3.cloned.1.call-done = bf16[2048,5248]{1,0:T(8,128)(2,1)} async-done(((bf16[64,5248]{1,0:T(8,128)(2,1)}), bf16[2048,5248]{1,0:T(8,128)(2,1)}) %all-gather.3.cloned.1.call-update) | async-done | bytes 21495824 | tf_op jit(solution)/shard_map/all_gather | solution.py:47
  215.0 0.0 copy-done
  215.0 1.5 fusion.9
  216.6 0.0 copy-start.1
  216.6 12.6 %fusion.18 = (f32[2048]{0:T(1024)S(1)}, f32[2048,304]{0,1:T(8,128)S(1)}) fusion(f32[2048,304]{0,1:T(8,128)S(1)} %fusion.9, f32[304,5120]{1,0:T(8,128)} %param.11, bf16[2048,5248]{1,0:T(8,128)(2,1)} %all-gather.3.cloned.1.call-done), kind=kOutput, calls=%fused_computation.33 | convolution fusion | flops 6378141696 | bytes 32186368 | tf_op jit(solution)/shard_map/dot_general | solution.py:17
  229.2 78.5 %pmax.7 = f32[2048]{0:T(1024)S(1)} all-reduce(f32[2048]{0:T(1024)S(1)} %get-tuple-element.6), channel_id=1, replica_groups=mesh['pop'=32,'tp'=8] {'pop','tp'}, use_global_device_ids=true, to_apply=%region_6.7 | all-reduce | flops 2048 | bytes 16384 | tf_op jit(solution)/shard_map/pmax | solution.py:55
  307.8 0.0 copy-done.1
  307.8 0.6 select_reduce_fusion
  308.4 72.7 %all-reduce = (f32[2048]{0:T(1024)S(1)}, f32[2048]{0:T(1024)S(1)}) all-reduce(f32[2048]{0:T(1024)S(1)} %get-tuple-element.3, f32[2048]{0:T(1024)S(1)} %get-tuple-element.2), channel_id=1, replica_groups=mesh['pop'=32,'tp'=8] {'pop','tp'}, use_global_device_ids=true, to_apply=%region_8.9 | all-reduce | flops 4096 | bytes 32768 | tf_op jit(solution)/shard_map/psum | solution.py:57
  381.1 0.1 reshape.41
  381.1 0.1 reduce_sum.39
  381.3 0.0 copy-start.2
  381.3 0.1 slice.14
  381.4 0.1 slice.15
  381.5 0.1 broadcast_in_dim.25
  381.6 0.1 mul.72
  381.7 0.0 all-gather.5.cloned.1.call-done
  381.7 6.8 %fusion.2 = f32[304,5120]{1,0:T(8,128)} fusion(f32[304,5120]{1,0:T(8,128)} %param.11, bf16[5120,128]{1,0:T(8,128)(2,1)} %all-gather.5.cloned.1.call-done, bf16[304,128]{1,0:T(8,128)(2,1)S(1)} %copy-done, f32[128]{0:T(128)S(1)} %mul.72), kind=kOutput, calls=%fused_computation.3 | convolution fusion | flops 401688576 | bytes 13840896 | tf_op jit(solution)/shard_map/dot_general | solution.py:17
  388.6 0.0 copy-done.2
  (9 shorter events, 0.1 us)
Async XLA Ops:
  7.2 207.9 %copy-start = (bf16[304,128]{1,0:T(8,128)(2,1)S(1)}, bf16[304,128]{1,0:T(8,128)(2,1)}, u32[]{:S(2)}) copy-start(bf16[304,128]{1,0:T(8,128)(2,1)} %param.9) | copy-start | bytes 233476
  7.2 207.9 %all-gather.3.cloned.1.call-start = ((), (), s32[]{:S(2)}) async-start(), calls=%async_computation | async-start | bytes 22167552 | tf_op jit(solution)/shard_map/all_gather | solution.py:47
  78.7 303.1 %all-gather.5.cloned.1.call-start = ((), (), s32[]{:S(2)}) async-start(), calls=%async_computation.1 | async-start | bytes 1474560 | tf_op jit(solution)/shard_map/all_gather | solution.py:44
  216.6 91.2 %copy-start.1 = (s32[2048]{0:T(1024)S(1)}, s32[2048]{0:T(1024)}, u32[]{:S(2)}) copy-start(s32[2048]{0:T(1024)} %param.10) | copy-start | bytes 24580
  381.3 7.3 %copy-start.2 = (f32[64]{0:T(128)}, f32[64]{0:T(128)S(1)}, u32[]{:S(2)}) copy-start(f32[64]{0:T(128)S(1)} %broadcast_multiply_fusion.1) | copy-start | bytes 772
Sparse Core Ops, SparseCore 0:
  78.8 136.1 all-gather.2
  217.6 52.0 all-gather.4
where the time goes:
time: 396 us; the launch traced here: 395 us
  blocking collectives  218 us (55%)
  waiting for transfers between devices  136 us (34%)
  matrix products  22.2 us (6%)
  between operations  14.2 us (4%)
    all_gather x1, waiting for transfers between devices, body(): piece = lax.all_gather(joined_rows, 'pop', axis=0, tiled=True)  136 us
    pmax x1, blocking collectives, body(): all_max = lax.pmax(row_max, ('pop', 'tp'))  78.5 us
    psum x1, blocking collectives, body(): all_sum, all_target = lax.psum((row_sum, target_logit), ('pop', 'tp'))  72.7 us
    all_gather x1, blocking collectives, body(): lax.all_gather(normed, 'tp', axis=1, tiled=True)  29.9 us
    psum x1, blocking collectives, body(): squares = lax.psum(jnp.sum(values * values, axis=1), 'tp')  21.5 us
    dot_general x3, matrix products, contract(): lax.dot_general(left, right, (((1,), (1,)), ((), ())), preferred_element_...  21 us
    psum x1, blocking collectives, body(): projection = lax.psum(partial_proj, 'tp')  15.7 us
  transfers between devices with their start and end apart: 2, of which 1 were waited for; matrix products, arithmetic and copies ran while one was open for 4% of the time, Pallas kernels for 0%

commit v1 on v0

v1 whole, which is shorter than its diff:
```python
import jax
import jax.numpy as jnp
from jax import lax
from jax.experimental import pallas as pl
from jax.experimental.pallas import tpu as pltpu
from jax.sharding import PartitionSpec as P

D = 5120
RANK = 4
NORM_EPS = 1e-06
SIGMA_NOISE = 0.25
LEARN_RATE = 0.5
NX, NY, NZ = 4, 4, 8
ROWS = 64
FEAT = 640
WA, WB = 128, 256
VOC = 304
FACT = 128
AUG = VOC + FACT
F32, BF16 = jnp.float32, jnp.bfloat16
MESH_ID = pl.DeviceIdType.MESH
NT = (((1,), (1,)), ((), ()))


class Ids:
    def __init__(self):
        self.table = {}

    def __call__(self, *key):
        return self.table.setdefault(key, len(self.table))


def message_names():
    ids = Ids()
    for d in range(1, 8):
        ids("sq", d)
    for d in range(1, 4):
        for kind in ("Rt", "B1", "C1", "A1", "A2"):
            ids(kind, d)
    ids("Rx")
    ids("Rd")
    for part in "ABC":
        for s in range(1, 5):
            ids("z", part, "up", s)
            if s < 4:
                ids("z", part, "dn", s)
    for k in range(8):
        for part in "BC":
            for way in ("up", "dn", "opp"):
                ids("last", part, k, way)
        for part in "ABC":
            ids("core", part, k)
    for d in range(1, 16):
        for stage in (1, 2, 3):
            ids("stat", stage, d)
    return ids


IDS = message_names()
N_MSG = len(IDS.table)


def combine(stats):
    top = stats[:, 0, :]
    best = jnp.max(top, axis=0, keepdims=True)
    total = jnp.sum(stats[:, 1, :] * jnp.exp(top - best), axis=0, keepdims=True)
    target = jnp.sum(stats[:, 2, :], axis=0, keepdims=True)
    return best, total, target


def gather_kernel(
    hid_ref, gain_ref, right_ref, left_ref, tgt_ref, master_ref,
    out_ref, rt_out_ref,
    buf_a, buf_b, buf_c, head_a, head_b, head_c, rt, stage, sq, st, r1, r2, r3,
    ssem, rsem, lsem,
):
    pop, tp = lax.axis_index("pop"), lax.axis_index("tp")
    c = lax.rem(pop, 2)
    z = lax.rem(lax.div(pop, 2), NZ)
    x_lo = lax.div(pop, 2 * NZ)
    x_hi = lax.div(tp, NY)
    y = lax.rem(tp, NY)
    x = x_hi * 2 + x_lo
    sib = 1 - c
    sgn = 1 - 2 * c

    def dev(xx, yy, zz, cc):
        return ((lax.rem(xx, 2) * NZ + zz) * 2 + cc, lax.div(xx, 2) * NY + yy)

    def off(v, k, n):
        return lax.rem(v + k * sgn + n, n)

    def plus(v, k, n):
        return lax.rem(v + k + n, n)

    sent = []

    def send(key, src, dst, device):
        i = IDS(*key)
        copy = pltpu.make_async_remote_copy(
            src_ref=src, dst_ref=dst, send_sem=ssem.at[i], recv_sem=rsem.at[i],
            device_id=device, device_id_type=MESH_ID,
        )
        copy.start()
        sent.append(copy)

    def recv(key, dst, device):
        i = IDS(*key)
        pltpu.make_async_remote_copy(
            src_ref=dst, dst_ref=dst, send_sem=ssem.at[i], recv_sem=rsem.at[i],
            device_id=device, device_id_type=MESH_ID,
        ).wait_recv()

    load = pltpu.make_async_copy(master_ref, stage, lsem.at[0])
    load.start()

    blk = x_lo * NZ + z
    quad = c * 8 + tp

    def blk_dev(b):
        return dev(x_hi * 2 + lax.div(b, NZ), y, lax.rem(b, NZ), c)

    def quad_dev(q):
        t = lax.rem(q, 8)
        return dev(lax.div(t, NY) * 2 + x_lo, lax.rem(t, NY), z, lax.div(q, 8))

    mirror = dev(3 - x, y, z, c)

    barrier = pltpu.get_barrier_semaphore()
    for d in range(1, 16):
        pl.semaphore_signal(barrier, inc=1, device_id=blk_dev(plus(blk, d, 16)), device_id_type=MESH_ID)
        pl.semaphore_signal(barrier, inc=1, device_id=quad_dev(plus(quad, d, 16)), device_id_type=MESH_ID)
    pl.semaphore_signal(barrier, inc=1, device_id=mirror, device_id_type=MESH_ID)

    values = hid_ref[...].astype(F32)
    squares = values * values
    folded = squares[:, 0:128]
    for j in range(1, FEAT // 128):
        folded = folded + squares[:, j * 128:(j + 1) * 128]
    folded = jnp.concatenate([folded, jnp.zeros((128 - ROWS, 128), F32)], axis=0)
    row_sq = jnp.sum(folded.T, axis=0, keepdims=True)
    sq[pl.ds(tp, 1)] = jnp.broadcast_to(row_sq, (8, 128))[None]
    for j in range(FEAT // 128):
        block_t = right_ref[j * 128:(j + 1) * 128, :].astype(F32).T.astype(BF16)
        rt[c, pl.ds(tp, 1), :, j * 128:(j + 1) * 128] = jnp.where(c == 0, block_t[:64], block_t[64:])[None]

    pl.semaphore_wait(barrier, 31)

    for d in range(1, 8):
        t = plus(tp, d, 8)
        send(("sq", d), sq.at[tp], sq.at[tp], dev(lax.div(t, NY) * 2 + x_lo, lax.rem(t, NY), z, c))
    for d in range(1, 4):
        send(("Rt", d), rt.at[c, tp], rt.at[c, tp], dev(x, plus(y, d, NY), z, c))
    for d in range(1, 8):
        t = plus(tp, -d, 8)
        recv(("sq", d), sq.at[t], dev(lax.div(t, NY) * 2 + x_lo, lax.rem(t, NY), z, c))

    row_scale = lax.rsqrt(jnp.sum(sq[:, 0, :], axis=0, keepdims=True) / D + NORM_EPS)
    scale = jnp.broadcast_to(row_scale, (128, 128)).T[:ROWS, :]
    scaled = jnp.concatenate(
        [values[:, j * 128:(j + 1) * 128] * scale for j in range(FEAT // 128)], axis=1
    )
    normed = (scaled * gain_ref[...]).astype(BF16)
    buf_b[z, c, y, x] = normed[:, WA:WA + WB]
    buf_c[z, c, x, y] = normed[:, WA + WB:]
    buf_a[z, c, y, x] = normed[:, :WA]

    for d in (1, 3, 2):
        send(("B1", d), buf_b.at[z, c, y, x], buf_b.at[z, c, y, x], dev(plus(x, d, NX), y, z, c))
        send(("C1", d), buf_c.at[z, c, x, y], buf_c.at[z, c, x, y], dev(x, plus(y, d, NY), z, c))
    for d in (1, 3, 2):
        send(("A1", d), buf_a.at[z, c, y, x], buf_a.at[z, c, y, x], dev(plus(x, d, NX), y, z, c))

    def z_dev(k):
        return dev(x, y, off(z, k, NZ), c)

    def y_dev(k):
        return dev(x, off(y, k, NY), z, c)

    def x_dev(k):
        return dev(off(x, k, NX), y, z, c)

    def blk_a(zz):
        return buf_a.at[zz, c]

    def blk_b(zz, yy):
        return buf_b.at[zz, c, yy]

    def blk_c(zz, xx):
        return buf_c.at[zz, c, xx]

    def z_blk(part, zz):
        return {"A": lambda: blk_a(zz), "B": lambda: blk_b(zz, y), "C": lambda: blk_c(zz, x)}[part]()

    slots = {0: [(0, "own", 0)], 4: [(7, "up", 4)]}
    for s in (1, 2, 3):
        slots[s] = [(2 * s - 1, "up", s), (2 * s, "dn", s)]

    def slot_z(way, s, orient=1):
        return off(z, -orient * s if way == "up" else orient * s, NZ)

    def last_send(part, k, zz):
        if part == "B":
            send(("last", part, k, "up"), blk_b(zz, y), blk_b(zz, y), y_dev(1))
            send(("last", part, k, "dn"), blk_b(zz, y), blk_b(zz, y), y_dev(-1))
        else:
            send(("last", part, k, "up"), blk_c(zz, x), blk_c(zz, x), x_dev(1))
            send(("last", part, k, "dn"), blk_c(zz, x), blk_c(zz, x), x_dev(-1))

    def z_start(part):
        send(("z", part, "up", 1), z_blk(part, z), z_blk(part, z), z_dev(1))
        send(("z", part, "dn", 1), z_blk(part, z), z_blk(part, z), z_dev(-1))

    def z_recv(s):
        for part in ("B", "C", "A"):
            for k, way, _ in slots[s]:
                zz = slot_z(way, s)
                step = 1 if way == "up" else -1
                recv(("z", part, way, s), z_blk(part, zz), z_dev(-step))
                if s < (4 if way == "up" else 3):
                    send(("z", part, way, s + 1), z_blk(part, zz), z_blk(part, zz), z_dev(step))
                if part != "A":
                    last_send(part, k, zz)

    def y_recv(s):
        for k, way, _ in slots[s]:
            zz = slot_z(way, s)
            below = blk_b(zz, off(y, -1, NY))
            recv(("last", "B", k, "up"), below, y_dev(-1))
            send(("last", "B", k, "opp"), below, below, y_dev(1))
            below = blk_c(zz, off(x, -1, NX))
            recv(("last", "C", k, "up"), below, x_dev(-1))
            send(("last", "C", k, "opp"), below, below, x_dev(1))

    def core_send(part, k, ref, zz):
        send(("core", part, k), ref.at[zz, c], ref.at[zz, c], dev(x, y, z, sib))

    def o_recv(s):
        for k, way, _ in slots[s]:
            zz = slot_z(way, s)
            core_send("A", k, buf_a, zz)
            recv(("last", "B", k, "dn"), blk_b(zz, off(y, 1, NY)), y_dev(1))
            recv(("last", "B", k, "opp"), blk_b(zz, off(y, 2, NY)), y_dev(-1))
            core_send("B", k, buf_b, zz)
            recv(("last", "C", k, "dn"), blk_c(zz, off(x, 1, NX)), x_dev(1))
            recv(("last", "C", k, "opp"), blk_c(zz, off(x, 2, NX)), x_dev(-1))
            core_send("C", k, buf_c, zz)

    def fill_head(lo, hi, source):
        for t in range(8):
            hi_t, y_t = divmod(t, NY)
            j = y_t * 2 + hi_t
            tile = source(t)
            head_a[lo:hi, j * WA:(j + 1) * WA] = tile[:, :WA]
            head_b[lo:hi, j * WB:(j + 1) * WB] = tile[:, WA:WA + WB]
            head_c[lo:hi, j * WB:(j + 1) * WB] = tile[:, WA + WB:]

    offset = (pop * 8 + tp) * VOC

    def compute_one(zz):
        def tokens(piece):
            return jnp.concatenate(
                [
                    jnp.concatenate([piece(cc, yy, hi * 2 + lo) for lo in range(2) for cc in range(2)], axis=0)
                    for yy in range(NY)
                    for hi in range(2)
                ],
                axis=1,
            )

        full = lax.dot_general(
            head_b[...], tokens(lambda cc, yy, xx: buf_b[zz, cc, yy, xx]), NT, preferred_element_type=F32
        )
        full += lax.dot_general(
            head_c[...], tokens(lambda cc, yy, xx: buf_c[zz, cc, xx, yy]), NT, preferred_element_type=F32
        )
        full += lax.dot_general(
            head_a[...], tokens(lambda cc, yy, xx: buf_a[zz, cc, yy, xx]), NT, preferred_element_type=F32
        )
        lane = lax.broadcasted_iota(jnp.int32, (FACT, 256), 1)
        column = lax.broadcasted_iota(jnp.int32, (FACT, 256), 0)
        lane_lo = lax.shift_right_logical(lane, 7)
        lane_c = lax.bitwise_and(lax.shift_right_logical(lane, 6), 1)
        pair = (lane_lo * NZ + zz) * 2 + lane_c
        odd = lax.bitwise_and(lax.shift_right_logical(lane, 5), 1)
        own = lax.shift_right_logical(column, 2) == pair
        sign = jnp.where(odd == 0, SIGMA_NOISE, -SIGMA_NOISE)
        lowrank = jnp.where(own, full[VOC:] * sign, 0.0).astype(BF16)
        logits = full[:VOC] + jnp.dot(left_ref[...], lowrank, preferred_element_type=F32)
        best = jnp.max(logits, axis=0, keepdims=True)
        total = jnp.sum(jnp.exp(logits - best), axis=0, keepdims=True)
        wanted = jnp.concatenate([tgt_ref[zz], tgt_ref[NZ + zz]], axis=1) - offset
        rows = lax.broadcasted_iota(jnp.int32, (VOC, 256), 0)
        target = jnp.sum(jnp.where(rows == wanted, logits, 0.0), axis=0, keepdims=True)
        packed = jnp.concatenate([best, total, target, jnp.zeros((5, 256), F32)], axis=0)
        st[zz, 0] = packed[:, :128]
        st[zz, 1] = packed[:, 128:]

    def compute(s):
        for k, way, _ in slots[s]:
            zz = slot_z(way, s, -1)
            for part, ref in (("A", buf_a), ("B", buf_b), ("C", buf_c)):
                recv(("core", part, k), ref.at[zz, sib], dev(x, y, z, sib))
        def body(i, carry):
            compute_one(off(z, -s + 2 * s * i, NZ))
            return carry

        lax.fori_loop(0, len(slots[s]), body, 0)

    for d in (1, 3, 2):
        src_x, src_y = plus(x, -d, NX), plus(y, -d, NY)
        recv(("B1", d), buf_b.at[z, c, y, src_x], dev(src_x, y, z, c))
        recv(("C1", d), buf_c.at[z, c, x, src_y], dev(x, src_y, z, c))
    z_start("B")
    z_start("C")
    last_send("B", 0, z)
    last_send("C", 0, z)
    for d in (1, 3, 2):
        src_x = plus(x, -d, NX)
        recv(("A1", d), buf_a.at[z, c, y, src_x], dev(src_x, y, z, c))
    for d in (1, 3, 2):
        send(("A2", d), buf_a.at[z, c, y], buf_a.at[z, c, y], dev(x, plus(y, d, NY), z, c))
    for d in range(1, 4):
        src_y = plus(y, -d, NY)
        recv(("Rt", d), rt.at[c, x_hi * NY + src_y], dev(x, src_y, z, c))
    send(("Rx",), rt.at[c, pl.ds(x_hi * NY, NY)], rt.at[c, pl.ds(x_hi * NY, NY)], mirror)

    load.wait()
    fill_head(0, VOC, lambda t: stage[:, t * FEAT:(t + 1) * FEAT].astype(BF16))

    for d in (1, 3, 2):
        src_y = plus(y, -d, NY)
        recv(("A2", d), buf_a.at[z, c, src_y], dev(x, src_y, z, c))
    z_start("A")

    z_recv(1)
    recv(("Rx",), rt.at[c, pl.ds((1 - x_hi) * NY, NY)], mirror)
    send(("Rd",), rt.at[c], rt.at[c], dev(x, y, z, sib))
    y_recv(0)
    z_recv(2)
    y_recv(1)
    o_recv(0)
    z_recv(3)
    y_recv(2)
    o_recv(1)
    recv(("Rd",), rt.at[sib], dev(x, y, z, sib))
    rt_copy = pltpu.make_async_copy(rt, rt_out_ref, lsem.at[1])
    rt_copy.start()
    fill_head(VOC, VOC + 64, lambda t: rt[0, t])
    fill_head(VOC + 64, AUG, lambda t: rt[1, t])
    compute(0)
    z_recv(4)
    y_recv(3)
    o_recv(2)
    compute(1)
    y_recv(4)
    o_recv(3)
    compute(2)
    compute(3)
    o_recv(4)
    compute(4)

    r1[pl.ds(blk, 1)] = st[z, x_lo][None]
    for d in range(1, 16):
        b = plus(blk, d, 16)
        send(("stat", 1, d), st.at[lax.rem(b, NZ), lax.div(b, NZ)], r1.at[blk], blk_dev(b))
    for d in range(1, 16):
        b = plus(blk, -d, 16)
        recv(("stat", 1, d), r1.at[b], blk_dev(b))
    best, total, target = combine(r1[...])
    packed = jnp.concatenate([best, total, target, jnp.zeros((5, 128), F32)], axis=0)
    r2[pl.ds(quad, 1)] = packed[None]
    for d in range(1, 16):
        send(("stat", 2, d), r2.at[quad], r2.at[quad], quad_dev(plus(quad, d, 16)))
    for d in range(1, 16):
        q = plus(quad, -d, 16)
        recv(("stat", 2, d), r2.at[q], quad_dev(q))
    best, total, target = combine(r2[...])
    logprob = target - best - jnp.log(total)
    lane = lax.broadcasted_iota(jnp.int32, (1, 128), 1)
    zero = jnp.zeros((1, 128), F32)
    means = [
        jnp.sum(jnp.where(lax.shift_right_logical(lane, 5) == m, logprob, 0.0), axis=1, keepdims=True) / 32.0
        for m in range(4)
    ]
    loglik, weights = zero, zero
    for m in range(4):
        loglik = jnp.where(lane == blk * 4 + m, means[m], loglik)
    for h in range(2):
        weights = jnp.where(lax.shift_right_logical(lane, 2) == blk * 2 + h, means[2 * h] - means[2 * h + 1], weights)
    packed = jnp.concatenate([loglik, weights, jnp.zeros((6, 128), F32)], axis=0)
    r3[pl.ds(blk, 1)] = packed[None]
    for d in range(1, 16):
        send(("stat", 3, d), r3.at[blk], r3.at[blk], blk_dev(plus(blk, d, 16)))
    for d in range(1, 16):
        b = plus(blk, -d, 16)
        recv(("stat", 3, d), r3.at[b], blk_dev(b))
    out_ref[...] = jnp.sum(r3[...], axis=0)
    for copy in sent:
        copy.wait_send()
    rt_copy.wait()


def update_kernel(w_ref, left_ref, rt_ref, master_ref, out_ref):
    scaled = (left_ref[...].astype(F32) * w_ref[1:2, :]).astype(BF16)
    right = jnp.concatenate([rt_ref[0, 0], rt_ref[1, 0]], axis=0)
    update = jnp.dot(scaled, right, preferred_element_type=F32)
    out_ref[...] = master_ref[...] + LEARN_RATE * update


def body(hidden, norm_gain, right_factors, left_factors, targets, master):
    vmem = pl.BlockSpec(memory_space=pltpu.VMEM)
    hbm = pl.BlockSpec(memory_space=pl.ANY)
    result, right_t = pl.pallas_call(
        gather_kernel,
        out_shape=(
            jax.ShapeDtypeStruct((8, 128), F32),
            jax.ShapeDtypeStruct((2, 8, 64, FEAT), BF16),
        ),
        in_specs=[vmem, vmem, vmem, vmem, vmem, hbm],
        out_specs=(vmem, hbm),
        scratch_shapes=[
            pltpu.VMEM((NZ, 2, NY, NX, ROWS, WA), BF16),
            pltpu.VMEM((NZ, 2, NY, NX, ROWS, WB), BF16),
            pltpu.VMEM((NZ, 2, NX, NY, ROWS, WB), BF16),
            pltpu.VMEM((AUG, 8 * WA), BF16),
            pltpu.VMEM((AUG, 8 * WB), BF16),
            pltpu.VMEM((AUG, 8 * WB), BF16),
            pltpu.VMEM((2, 8, 64, FEAT), BF16),
            pltpu.VMEM((VOC, D), F32),
            pltpu.VMEM((8, 8, 128), F32),
            pltpu.VMEM((NZ, 2, 8, 128), F32),
            pltpu.VMEM((16, 8, 128), F32),
            pltpu.VMEM((16, 8, 128), F32),
            pltpu.VMEM((16, 8, 128), F32),
            pltpu.SemaphoreType.DMA((N_MSG,)),
            pltpu.SemaphoreType.DMA((N_MSG,)),
            pltpu.SemaphoreType.DMA((2,)),
        ],
        compiler_params=pltpu.CompilerParams(
            collective_id=0, has_side_effects=True, vmem_limit_bytes=56 * 1024 * 1024
        ),
        name="gather_logits",
    )(
        hidden, norm_gain.reshape(1, FEAT), right_factors, left_factors,
        targets.reshape(16, 1, 128), master,
    )
    new_master = pl.pallas_call(
        update_kernel,
        out_shape=jax.ShapeDtypeStruct((VOC, D), F32),
        grid=(8,),
        in_specs=[
            pl.BlockSpec((8, 128), lambda i: (0, 0)),
            pl.BlockSpec((VOC, FACT), lambda i: (0, 0)),
            pl.BlockSpec((2, 1, 64, FEAT), lambda i: (0, i, 0, 0)),
            pl.BlockSpec((VOC, FEAT), lambda i: (0, i)),
        ],
        out_specs=pl.BlockSpec((VOC, FEAT), lambda i: (0, i)),
        name="update_master",
    )(result, left_factors, right_t, master)
    return (result[0, :64], new_master)


def solution(mesh):
    in_specs = (
        P("pop", "tp"),
        P("tp"),
        P("tp", None),
        P(("pop", "tp"), None),
        P(),
        P(("pop", "tp"), None),
    )
    out_specs = (P(), P(("pop", "tp"), None))
    return jax.shard_map(body, mesh=mesh, in_specs=in_specs, out_specs=out_specs, check_vma=False)
```

time: 396 us -> 111 us (0.28)
  blocking collectives: 218 us -> 0 us
  waiting for transfers between devices: 136 us -> 0 us
  Pallas kernels: 0 us -> 107 us
  matrix products: 22.2 us -> 0 us
  between operations: 14.2 us -> 0.64 us
    all_gather x2 -> x0, waiting for transfers between devices: 136 us -> none  [the longest x1 136 us: body(): piece = lax.all_gather(joined_rows, 'pop', axis=0, tiled=True)]
    psum x3 -> x0, blocking collectives: 110 us -> none  [the longest x1 72.7 us: body(): all_sum, all_target = lax.psum((row_sum, target_logit), ('pop', 'tp'))]
    pallas_call x0 -> x2, Pallas kernels: none -> 107 us  [the longest x1 98.5 us: body(): pl.pallas_call(gather_kernel, out_shape=(jax.ShapeDtypeStruct((8, 128), F...]
    pmax x1 -> x0, blocking collectives: 78.5 us -> none  [body(): all_max = lax.pmax(row_max, ('pop', 'tp'))]
    all_gather x1 -> x0, blocking collectives: 29.9 us -> none  [body(): lax.all_gather(normed, 'tp', axis=1, tiled=True)]
    dot_general x4 -> x0, matrix products: 22.2 us -> none  [the longest x3 21 us: contract(): lax.dot_general(left, right, (((1,), (1,)), ((), ())), preferred_element_...]
  transfers between devices with their start and end apart: 2 -> 0, of which waited for: 1 -> 0; matrix products, arithmetic and copies ran while one was open for 4% -> 0% of each run, Pallas kernels for 0% -> 0%
where the time goes in v1:
time: 111 us; the launch traced here: 110 us
  Pallas kernels  107 us (96%)
  local copies, waits for them, and re-layouts  2.45 us (2%)
    pallas_call x1, Pallas kernels, body(): pl.pallas_call(gather_kernel, out_shape=(jax.ShapeDtypeStruct((8, 128), F...  98.5 us
    pallas_call x1, Pallas kernels, body(): pl.pallas_call(update_kernel, out_shape=jax.ShapeDtypeStruct((VOC, D), F3...  8.88 us

profile of v1, /device:TPU:1, one launch (start us, length us, event | category | flops | bytes accessed | tf_op | source)
XLA Modules:
  0.0 110.4 jit_solution(1755646569530582569)
XLA Ops:
  0.6 1.3 %reshape.10.gain_ref = f32[1,640]{1,0:T(1,128)} reshape(f32[640]{0:T(1024)} %param.7) | data formatting | bytes 5120 | tf_op jit(solution)/shard_map/reshape | solution.py:445
  1.9 98.5 %gather_logits.1 = (f32[8,128]{1,0:T(8,128)}, bf16[2,8,64,640]{3,2,1,0:T(8,128)(2,1)}) custom-call(bf16[64,640]{1,0:T(8,128)(2,1)} %hid_ref.1, f32[1,640]{1,0:T(1,128)} %reshape.10.gain_ref, bf16[640,128]{1,0:T(8,128)(2,1)} %right_ref.1, bf16[304,128]{1,0:T(8,128)(2,1)} %left_ref.3, s32[16,1,128]{2,1,0:T(1,128)} %bitcast.3, f32[304,5120]{1,0:T(8,128)} %master_ref.3), custom_call_target="tpu_custom_call" | custom-call | tf_op jit(solution)/shard_map/gather_logits/pallas_call | solution.py:414
  100.4 8.9 %update_master.1 = f32[304,5120]{1,0:T(8,128)} custom-call(f32[8,128]{1,0:T(8,128)} %get-tuple-element.4.w_ref, bf16[304,128]{1,0:T(8,128)(2,1)} %left_ref.3, bf16[2,8,64,640]{3,2,1,0:T(8,128)(2,1)} %get-tuple-element.5.rt_ref, f32[304,5120]{1,0:T(8,128)} %master_ref.3), custom_call_target="tpu_custom_call" | custom-call | tf_op jit(solution)/shard_map/update_master/pallas_call | solution.py:448
  109.2 1.2 %slice_bitcast_fusion = f32[64]{0:T(128)} fusion(f32[8,128]{1,0:T(8,128)} %get-tuple-element.4.w_ref), kind=kLoop, calls=%fused_computation | loop fusion | bytes 512 | tf_op jit(solution)/shard_map/squeeze | solution.py:461

commit v2 on v1

v2 whole, which is shorter than its diff:
```python
import jax
import jax.numpy as jnp
from jax import lax
from jax.experimental import pallas as pl
from jax.experimental.pallas import tpu as pltpu
from jax.sharding import PartitionSpec as P

D = 5120
RANK = 4
NORM_EPS = 1e-06
SIGMA_NOISE = 0.25
LEARN_RATE = 0.5
NX, NY, NZ = 4, 4, 8
ROWS = 64
FEAT = 640
WA, WB = 128, 256
VOC = 304
FACT = 128
AUG = VOC + FACT
F32, BF16 = jnp.float32, jnp.bfloat16
MESH_ID = pl.DeviceIdType.MESH
NT = (((1,), (1,)), ((), ()))


class Ids:
    def __init__(self):
        self.table = {}

    def __call__(self, *key):
        return self.table.setdefault(key, len(self.table))


SLOTS = {0: [(0, "own", 0)], 4: [(7, "up", 4)]}
for _s in (1, 2, 3):
    SLOTS[_s] = [(2 * _s - 1, "up", _s), (2 * _s, "dn", _s)]
FINE = (5, 6, 7)


def message_names():
    ids = Ids()
    for dx in range(4):
        for dy in range(4):
            ids("sq", dx, dy)
    for d in range(1, 4):
        for kind in ("Rt", "B1", "C1", "A1", "A2"):
            ids(kind, d)
    ids("Rx")
    ids("Rd")
    for part in "ABC":
        for s in range(1, 5):
            ids("z", part, "up", s)
            if s < 4:
                ids("z", part, "dn", s)
    for k in range(8):
        for part in "BC":
            for way in ("up", "dn", "opp"):
                ids("last", part, k, way)
        for part in "ABC":
            if part != "A" and k in FINE:
                for piece in range(4):
                    ids("core", part, k, piece)
            else:
                ids("core", part, k)
    for i in range(2):
        for k in range(8):
            ids("stat1", i, k)
            ids("stat3", i, k)
            ids("stat2", i, k)
    return ids


IDS = message_names()
N_MSG = len(IDS.table)


def combine(stats):
    top = stats[:, 0, :]
    best = jnp.max(top, axis=0, keepdims=True)
    total = jnp.sum(stats[:, 1, :] * jnp.exp(top - best), axis=0, keepdims=True)
    target = jnp.sum(stats[:, 2, :], axis=0, keepdims=True)
    return best, total, target


def gather_kernel(
    hid_ref, gain_ref, right_ref, left_ref, tgt_ref, master_ref,
    out_ref, stage, rt,
    buf_a, buf_b, buf_c, head_a, head_b, head_c, raw_a, raw_b, raw_c, sq, st, r1, r2, r3,
    ssem, rsem, lsem,
):
    pop, tp = lax.axis_index("pop"), lax.axis_index("tp")
    c = lax.rem(pop, 2)
    z = lax.rem(lax.div(pop, 2), NZ)
    x_lo = lax.div(pop, 2 * NZ)
    x_hi = lax.div(tp, NY)
    y = lax.rem(tp, NY)
    x = x_hi * 2 + x_lo
    sib = 1 - c
    sgn = 1 - 2 * c
    blk = x_lo * NZ + z
    quad = c * 8 + tp

    xs = [lax.rem(x + k, NX) for k in range(NX)]
    ys = [lax.rem(y + k, NY) for k in range(NY)]
    zs = {k: lax.rem(z + k * sgn + NZ, NZ) for k in range(-4, 8)}
    xo = {k: lax.rem(x + k * sgn + NX, NX) for k in (-1, 0, 1, 2)}
    yo = {k: lax.rem(y + k * sgn + NY, NY) for k in (-1, 0, 1, 2)}
    los = (x_lo, 1 - x_lo)

    def dev(xx, yy, zz, cc):
        return ((lax.rem(xx, 2) * NZ + zz) * 2 + cc, lax.div(xx, 2) * NY + yy)

    sent = []

    def send(key, src, dst, device):
        i = IDS(*key)
        copy = pltpu.make_async_remote_copy(
            src_ref=src, dst_ref=dst, send_sem=ssem.at[i], recv_sem=rsem.at[i],
            device_id=device, device_id_type=MESH_ID,
        )
        copy.start()
        sent.append(copy)

    def recv(key, dst, device):
        i = IDS(*key)
        pltpu.make_async_remote_copy(
            src_ref=dst, dst_ref=dst, send_sem=ssem.at[i], recv_sem=rsem.at[i],
            device_id=device, device_id_type=MESH_ID,
        ).wait_recv()

    mirror = dev(3 - x, y, z, c)
    sibling = dev(x, y, z, sib)

    def plane(dx, dy):
        return dev(xs[dx], ys[dy], z, c)

    PLANE = [(dx, dy) for dx in range(NX) for dy in range(NY) if dx or dy]

    barrier = pltpu.get_barrier_semaphore()
    for dx, dy in PLANE:
        pl.semaphore_signal(barrier, inc=1, device_id=plane(dx, dy), device_id_type=MESH_ID)
    for device in (dev(x, y, zs[1], c), dev(x, y, zs[-1], c), sibling):
        pl.semaphore_signal(barrier, inc=1, device_id=device, device_id_type=MESH_ID)

    load = pltpu.make_async_copy(master_ref, stage, lsem.at[0])
    load.start()

    raw_a[pl.ds(x, 1)] = hid_ref[:, :WA][None]
    raw_b[pl.ds(x, 1)] = hid_ref[:, WA:WA + WB][None]
    raw_c[pl.ds(y, 1)] = hid_ref[:, WA + WB:][None]
    folded = jnp.zeros((ROWS, 128), F32)
    for j in range(FEAT // 128):
        piece = hid_ref[:, j * 128:(j + 1) * 128].astype(F32)
        folded = folded + piece * piece
    folded = jnp.concatenate([folded, jnp.zeros((128 - ROWS, 128), F32)], axis=0)
    row_sq = jnp.sum(folded.T, axis=0, keepdims=True)
    gains = [gain_ref[pl.ds(j * 128, 128)].reshape(1, 128) for j in range(FEAT // 128)]
    packed = jnp.concatenate([row_sq] + gains + [jnp.zeros((2, 128), F32)], axis=0)
    sq[pl.ds(x, 1), pl.ds(y, 1)] = packed[None, None]
    for j in range(FEAT // 128):
        block_t = right_ref[j * 128:(j + 1) * 128, :].astype(F32).T.astype(BF16)
        rt[c, pl.ds(tp, 1), :, j * 128:(j + 1) * 128] = jnp.where(c == 0, block_t[:64], block_t[64:])[None]

    pl.semaphore_wait(barrier, len(PLANE) + 3)

    for d in (1, 3, 2):
        send(("B1", d), raw_b.at[x], raw_b.at[x], plane(d, 0))
        send(("C1", d), raw_c.at[y], raw_c.at[y], plane(0, d))
    for dx, dy in PLANE:
        send(("sq", dx, dy), sq.at[x, y], sq.at[x, y], plane(dx, dy))
    for d in (1, 3, 2):
        send(("A1", d), raw_a.at[x], raw_a.at[x], plane(d, 0))
    for d in (1, 3, 2):
        send(("Rt", d), rt.at[c, tp], rt.at[c, tp], plane(0, d))

    def z_dev(k):
        return dev(x, y, zs[k], c)

    def y_dev(k):
        return dev(x, yo[k], z, c)

    def x_dev(k):
        return dev(xo[k], y, z, c)

    def blk_a(zz):
        return buf_a.at[zz, c]

    def blk_b(zz, yy):
        return buf_b.at[zz, c, yy]

    def blk_c(zz, xx):
        return buf_c.at[zz, c, xx]

    def z_blk(part, zz):
        return blk_a(zz) if part == "A" else blk_b(zz, y) if part == "B" else blk_c(zz, x)

    def slot_z(way, s, orient=1):
        return zs[-orient * s if way == "up" else orient * s]

    def last_send(part, k, zz):
        block = z_blk(part, zz)
        there = y_dev if part == "B" else x_dev
        send(("last", part, k, "up"), block, block, there(1))
        send(("last", part, k, "dn"), block, block, there(-1))
        if k in FINE:
            send(("core", part, k, 0), block, block, sibling)

    def z_start(part):
        send(("z", part, "up", 1), z_blk(part, z), z_blk(part, z), z_dev(1))
        send(("z", part, "dn", 1), z_blk(part, z), z_blk(part, z), z_dev(-1))

    def z_recv(s, parts):
        for part in parts:
            for k, way, _ in SLOTS[s]:
                zz = slot_z(way, s)
                step = 1 if way == "up" else -1
                recv(("z", part, way, s), z_blk(part, zz), z_dev(-step))
                if s < (4 if way == "up" else 3):
                    send(("z", part, way, s + 1), z_blk(part, zz), z_blk(part, zz), z_dev(step))
                if part == "A":
                    send(("core", "A", k), blk_a(zz), blk_a(zz), sibling)
                else:
                    last_send(part, k, zz)

    def last_blk(part, zz, k):
        return blk_b(zz, yo[k]) if part == "B" else blk_c(zz, xo[k])

    def y_recv(s):
        for k, way, _ in SLOTS[s]:
            zz = slot_z(way, s)
            for part, there in (("B", y_dev), ("C", x_dev)):
                below = last_blk(part, zz, -1)
                recv(("last", part, k, "up"), below, there(-1))
                send(("last", part, k, "opp"), below, below, there(1))
                if k in FINE:
                    send(("core", part, k, 1), below, below, sibling)

    def o_recv(s):
        for k, way, _ in SLOTS[s]:
            zz = slot_z(way, s)
            for part, ref, there in (("B", buf_b, y_dev), ("C", buf_c, x_dev)):
                above, opposite = last_blk(part, zz, 1), last_blk(part, zz, 2)
                recv(("last", part, k, "dn"), above, there(1))
                if k in FINE:
                    send(("core", part, k, 2), above, above, sibling)
                recv(("last", part, k, "opp"), opposite, there(-1))
                if k in FINE:
                    send(("core", part, k, 3), opposite, opposite, sibling)
                else:
                    send(("core", part, k), ref.at[zz, c], ref.at[zz, c], sibling)

    def core_recv(s):
        for k, way, _ in SLOTS[s]:
            zz = slot_z(way, s, -1)
            recv(("core", "A", k), buf_a.at[zz, sib], sibling)
            for part, ref, other in (("B", buf_b, yo), ("C", buf_c, xo)):
                if k in FINE:
                    for piece, at in ((0, 0), (1, 1), (2, -1), (3, 2)):
                        recv(("core", part, k, piece), ref.at[zz, sib, other[at]], sibling)
                else:
                    recv(("core", part, k), ref.at[zz, sib], sibling)

    def fill_head(lo, hi, source):
        for t in range(8):
            hi_t, y_t = divmod(t, NY)
            j = y_t * 2 + hi_t
            tile = source(t)
            head_a[lo:hi, j * WA:(j + 1) * WA] = tile[:, :WA]
            head_b[lo:hi, j * WB:(j + 1) * WB] = tile[:, WA:WA + WB]
            head_c[lo:hi, j * WB:(j + 1) * WB] = tile[:, WA + WB:]

    offset = (pop * 8 + tp) * VOC

    def compute_one(zz):
        def tokens(piece):
            return jnp.concatenate(
                [
                    jnp.concatenate([piece(cc, yy, hi * 2 + lo) for lo in range(2) for cc in range(2)], axis=0)
                    for yy in range(NY)
                    for hi in range(2)
                ],
                axis=1,
            )

        full = lax.dot_general(
            head_b[...], tokens(lambda cc, yy, xx: buf_b[zz, cc, yy, xx]), NT, preferred_element_type=F32
        )
        full += lax.dot_general(
            head_c[...], tokens(lambda cc, yy, xx: buf_c[zz, cc, xx, yy]), NT, preferred_element_type=F32
        )
        full += lax.dot_general(
            head_a[...], tokens(lambda cc, yy, xx: buf_a[zz, cc, yy, xx]), NT, preferred_element_type=F32
        )
        lane = lax.broadcasted_iota(jnp.int32, (FACT, 256), 1)
        column = lax.broadcasted_iota(jnp.int32, (FACT, 256), 0)
        lane_lo = lax.shift_right_logical(lane, 7)
        lane_c = lax.bitwise_and(lax.shift_right_logical(lane, 6), 1)
        pair = (lane_lo * NZ + zz) * 2 + lane_c
        odd = lax.bitwise_and(lax.shift_right_logical(lane, 5), 1)
        own = lax.shift_right_logical(column, 2) == pair
        sign = jnp.where(odd == 0, SIGMA_NOISE, -SIGMA_NOISE)
        lowrank = jnp.where(own, full[VOC:] * sign, 0.0).astype(BF16)
        logits = full[:VOC] + jnp.dot(left_ref[...], lowrank, preferred_element_type=F32)
        best = jnp.max(logits, axis=0, keepdims=True)
        total = jnp.sum(jnp.exp(logits - best), axis=0, keepdims=True)
        wanted = jnp.concatenate([tgt_ref[zz], tgt_ref[NZ + zz]], axis=1) - offset
        rows = lax.broadcasted_iota(jnp.int32, (VOC, 256), 0)
        target = jnp.sum(jnp.where(rows == wanted, logits, 0.0), axis=0, keepdims=True)
        packed = jnp.concatenate([best, total, target, jnp.zeros((5, 256), F32)], axis=0)
        st[zz, 0] = packed[:, :128]
        st[zz, 1] = packed[:, 128:]

    def stat_send(k):
        for i in range(2):
            if i or k:
                send(("stat1", i, k % 8), st.at[zs[k], los[i]], r1.at[blk], dev(x_hi * 2 + los[i], y, zs[k], c))

    def compute(s):
        core_recv(s)

        def loop(i, carry):
            compute_one(lax.rem(z + (2 * i - 1) * s + NZ, NZ))
            return carry

        if s in (0, 4):
            compute_one(zs[s])
        else:
            lax.fori_loop(0, 2, loop, 0)
        stat_send(s)
        if s in (1, 2, 3):
            stat_send(8 - s)

    for dx, dy in PLANE:
        recv(("sq", dx, dy), sq.at[xs[-dx], ys[-dy]], plane(-dx, -dy))
    scales = []
    for lo in range(2):
        total = sq[lo, :, 0, :] + sq[lo + 2, :, 0, :]
        row_scale = lax.rsqrt(jnp.sum(total, axis=0, keepdims=True) / D + NORM_EPS)
        scales.append(jnp.broadcast_to(row_scale, (128, 128)).T[:ROWS, :])
    own_scale = jnp.where(x_lo == 0, scales[0], scales[1])

    def normalize(values, scale, xx, yy, first, count):
        return jnp.concatenate(
            [
                (values[:, j * 128:(j + 1) * 128].astype(F32) * scale * sq[xx, yy, 1 + first + j:2 + first + j, :]).astype(BF16)
                for j in range(count)
            ],
            axis=1,
        )

    for d in (1, 3, 2):
        recv(("B1", d), raw_b.at[xs[-d]], plane(-d, 0))
    for t in range(NX):
        buf_b[z, c, y, t] = normalize(raw_b[t], scales[t % 2], t, y, 1, 2)
    z_start("B")
    last_send("B", 0, z)
    for d in (1, 3, 2):
        recv(("C1", d), raw_c.at[ys[-d]], plane(0, -d))
    for t in range(NY):
        buf_c[z, c, x, t] = normalize(raw_c[t], own_scale, x, t, 3, 2)
    z_start("C")
    last_send("C", 0, z)
    for d in (1, 3, 2):
        recv(("A1", d), raw_a.at[xs[-d]], plane(-d, 0))
    for t in range(NX):
        buf_a[z, c, y, t] = normalize(raw_a[t], scales[t % 2], t, y, 0, 1)
    for d in (1, 3, 2):
        send(("A2", d), buf_a.at[z, c, y], buf_a.at[z, c, y], plane(0, d))
    for d in range(1, 4):
        recv(("Rt", d), rt.at[c, x_hi * NY + ys[-d]], plane(0, -d))
    send(("Rx",), rt.at[c, pl.ds(x_hi * NY, NY)], rt.at[c, pl.ds(x_hi * NY, NY)], mirror)

    load.wait()
    fill_head(0, VOC, lambda t: stage[:, t * FEAT:(t + 1) * FEAT].astype(BF16))

    z_recv(1, "BC")
    y_recv(0)
    z_recv(2, "BC")
    for d in (1, 3, 2):
        recv(("A2", d), buf_a.at[z, c, ys[-d]], plane(0, -d))
    z_start("A")
    send(("core", "A", 0), blk_a(z), blk_a(z), sibling)
    recv(("Rx",), rt.at[c, pl.ds((1 - x_hi) * NY, NY)], mirror)
    send(("Rd",), rt.at[c], rt.at[c], sibling)
    y_recv(1)
    o_recv(0)
    z_recv(3, "BC")
    z_recv(1, "A")
    y_recv(2)
    o_recv(1)
    recv(("Rd",), rt.at[sib], sibling)
    fill_head(VOC, VOC + 64, lambda t: rt[0, t])
    fill_head(VOC + 64, AUG, lambda t: rt[1, t])
    compute(0)
    z_recv(4, "BC")
    z_recv(2, "A")
    compute(1)
    y_recv(3)
    o_recv(2)
    z_recv(3, "A")
    compute(2)
    y_recv(4)
    o_recv(3)
    z_recv(4, "A")
    o_recv(4)
    compute(3)
    compute(4)

    r1[pl.ds(blk, 1)] = st[z, x_lo][None]
    for copy in sent:
        copy.wait_send()
    sent.clear()
    for k in range(8):
        for i in range(2):
            if i or k:
                recv(("stat1", i, k), r1.at[los[i] * NZ + zs[-k if k < 5 else 8 - k]], dev(x_hi * 2 + los[i], y, zs[-k if k < 5 else 8 - k], c))
    best, total, target = combine(r1[...])
    packed = jnp.concatenate([best, total, target, jnp.zeros((5, 128), F32)], axis=0)
    r2[pl.ds(quad, 1)] = packed[None]

    def quad_at(i, k):
        h, d = divmod(k, 4)
        hi = x_hi if h == 0 else 1 - x_hi
        cc = c if i == 0 else sib
        return cc, hi, d

    QUAD = [(i, k) for i in range(2) for k in range(8) if i or k]
    for i, k in QUAD:
        cc, hi, d = quad_at(i, k)
        send(("stat2", i, k), r2.at[quad], r2.at[quad], dev(hi * 2 + x_lo, ys[d], z, cc))
    for i, k in QUAD:
        cc, hi, d = quad_at(i, k)
        recv(("stat2", i, k), r2.at[cc * 8 + hi * NY + ys[-d]], dev(hi * 2 + x_lo, ys[-d], z, cc))
    best, total, target = combine(r2[...])
    logprob = target - best - jnp.log(total)
    lane = lax.broadcasted_iota(jnp.int32, (1, 128), 1)
    zero = jnp.zeros((1, 128), F32)
    means = [
        jnp.sum(jnp.where(lax.shift_right_logical(lane, 5) == m, logprob, 0.0), axis=1, keepdims=True) / 32.0
        for m in range(4)
    ]
    loglik, weights = zero, zero
    for m in range(4):
        loglik = jnp.where(lane == blk * 4 + m, means[m], loglik)
    for h in range(2):
        weights = jnp.where(lax.shift_right_logical(lane, 2) == blk * 2 + h, means[2 * h] - means[2 * h + 1], weights)
    packed = jnp.concatenate([loglik, weights, jnp.zeros((6, 128), F32)], axis=0)
    r3[pl.ds(blk, 1)] = packed[None]
    for i, k in QUAD:
        send(("stat3", i, k), r3.at[blk], r3.at[blk], dev(x_hi * 2 + los[i], y, zs[k], c))
    for i, k in QUAD:
        zz = zs[-k if k < 5 else 8 - k]
        recv(("stat3", i, k), r3.at[los[i] * NZ + zz], dev(x_hi * 2 + los[i], y, zz, c))
    out_ref[...] = jnp.sum(r3[...], axis=0)
    for copy in sent:
        copy.wait_send()


def update_kernel(w_ref, left_ref, rt_ref, master_ref, ll_ref, out_ref, block, sems):
    ll_ref[...] = w_ref[0, :64]
    scaled = (left_ref[...].astype(F32) * w_ref[1:2, :]).astype(BF16)
    copies = []
    for t in range(8):
        cols = slice(t * FEAT, (t + 1) * FEAT)
        right = jnp.concatenate([rt_ref[0, t], rt_ref[1, t]], axis=0)
        update = jnp.dot(scaled, right, preferred_element_type=F32)
        block[:, cols] = master_ref[:, cols] + LEARN_RATE * update
        copy = pltpu.make_async_copy(block.at[:, cols], out_ref.at[:, cols], sems.at[t])
        copy.start()
        copies.append(copy)
    for copy in copies:
        copy.wait()


def body(hidden, norm_gain, right_factors, left_factors, targets, master):
    vmem = pl.BlockSpec(memory_space=pltpu.VMEM)
    hbm = pl.BlockSpec(memory_space=pl.ANY)
    result, stage, right_t = pl.pallas_call(
        gather_kernel,
        out_shape=(
            pltpu.VMEM((8, 128), F32),
            pltpu.VMEM((VOC, D), F32),
            pltpu.VMEM((2, 8, 64, FEAT), BF16),
        ),
        in_specs=[vmem, vmem, vmem, vmem, vmem, hbm],
        out_specs=(vmem, vmem, vmem),
        scratch_shapes=[
            pltpu.VMEM((NZ, 2, NY, NX, ROWS, WA), BF16),
            pltpu.VMEM((NZ, 2, NY, NX, ROWS, WB), BF16),
            pltpu.VMEM((NZ, 2, NX, NY, ROWS, WB), BF16),
            pltpu.VMEM((AUG, 8 * WA), BF16),
            pltpu.VMEM((AUG, 8 * WB), BF16),
            pltpu.VMEM((AUG, 8 * WB), BF16),
            pltpu.VMEM((NX, ROWS, WA), BF16),
            pltpu.VMEM((NX, ROWS, WB), BF16),
            pltpu.VMEM((NY, ROWS, WB), BF16),
            pltpu.VMEM((NX, NY, 8, 128), F32),
            pltpu.VMEM((NZ, 2, 8, 128), F32),
            pltpu.VMEM((16, 8, 128), F32),
            pltpu.VMEM((16, 8, 128), F32),
            pltpu.VMEM((16, 8, 128), F32),
            pltpu.SemaphoreType.DMA((N_MSG,)),
            pltpu.SemaphoreType.DMA((N_MSG,)),
            pltpu.SemaphoreType.DMA((1,)),
        ],
        compiler_params=pltpu.CompilerParams(
            collective_id=0, has_side_effects=True, vmem_limit_bytes=40 * 1024 * 1024
        ),
        name="gather_logits",
    )(
        hidden, norm_gain, right_factors, left_factors,
        targets.reshape(16, 1, 128), master,
    )
    loglik, new_master = pl.pallas_call(
        update_kernel,
        out_shape=(jax.ShapeDtypeStruct((64,), F32), jax.ShapeDtypeStruct((VOC, D), F32)),
        in_specs=[vmem, vmem, vmem, vmem],
        out_specs=(vmem, hbm),
        scratch_shapes=[pltpu.VMEM((VOC, D), F32), pltpu.SemaphoreType.DMA((8,))],
        compiler_params=pltpu.CompilerParams(vmem_limit_bytes=20 * 1024 * 1024),
        name="update_master",
    )(result, left_factors, right_t, stage)
    return (loglik, new_master)


def solution(mesh):
    in_specs = (
        P("pop", "tp"),
        P("tp"),
        P("tp", None),
        P(("pop", "tp"), None),
        P(),
        P(("pop", "tp"), None),
    )
    out_specs = (P(), P(("pop", "tp"), None))
    return jax.shard_map(body, mesh=mesh, in_specs=in_specs, out_specs=out_specs, check_vma=False)
```

time: 111 us -> 98.2 us (0.88)
  Pallas kernels: 107 us -> 90.4 us
  local copies, waits for them, and re-layouts: 2.45 us -> 6.83 us
    pallas_call x2, Pallas kernels: 107 us -> 90.4 us  [the longest x1 86.9 us: body(): pl.pallas_call(gather_kernel, out_shape=(pltpu.VMEM((8, 128), F32), pltpu...]
    unnamed x0 -> x12, local copies, waits for them, and re-layouts: none -> 6.83 us
    reshape x1 -> x0, local copies, waits for them, and re-layouts: 1.27 us -> none  [body(): norm_gain.reshape(1, FEAT)]
    squeeze x1 -> x0, local copies, waits for them, and re-layouts: 1.18 us -> none  [body(): return (result[0, :64], new_master)]
where the time goes in v2:
time: 98.2 us; the launch traced here: 97.9 us
  Pallas kernels  90.4 us (92%)
  local copies, waits for them, and re-layouts  6.83 us (7%)
    pallas_call x1, Pallas kernels, body(): pl.pallas_call(gather_kernel, out_shape=(pltpu.VMEM((8, 128), F32), pltpu...  86.9 us
    unnamed x12, local copies, waits for them, and re-layouts  6.83 us
    pallas_call x1, Pallas kernels, body(): pl.pallas_call(update_kernel, out_shape=(jax.ShapeDtypeStruct((64,), F32)...  3.54 us

profile of v2, /device:TPU:1, one launch (start us, length us, event | category | flops | bytes accessed | tf_op | source)
XLA Modules:
  0.0 97.9 jit_solution(6430578911768897308)
XLA Ops:
  0.6 0.0 copy-start
  0.6 2.8 %copy-done = f32[304,5120]{1,0:T(8,128)S(1)} copy-done((f32[304,5120]{1,0:T(8,128)S(1)}, f32[304,5120]{1,0:T(8,128)}, u32[]{:S(2)}) %copy-start) | copy-done | bytes 6225944
  3.4 0.0 copy-start.1
  3.4 0.9 copy-done.1
  4.3 0.0 copy-start.2
  4.3 0.9 copy-done.2
  5.2 0.0 copy-start.3
  5.2 0.9 copy-done.3
  6.1 0.0 copy-start.4
  6.1 0.7 copy-done.4
  6.8 0.0 copy-start.5
  6.8 0.7 copy-done.5
  7.5 86.9 %gather_logits.1 = (f32[8,128]{1,0:T(8,128)S(1)}, f32[304,5120]{1,0:T(8,128)S(1)}, bf16[2,8,64,640]{3,2,1,0:T(8,128)(2,1)S(1)}) custom-call(bf16[64,640]{1,0:T(8,128)(2,1)S(1)} %copy-done.3, f32[640]{0:T(1024)S(1)} %copy-done.5, bf16[640,128]{1,0:T(8,128)(2,1)S(1)} %copy-done.2, bf16[304,128]{1,0:T(8,128)(2,1)S(1)} %copy-done.1, s32[16,1,128]{2,1,0:T(1,128)S(1)} %bitcast.1, ...), custom_call_target="tpu_custom_call" | custom-call | tf_op jit(solution)/shard_map/gather_logits/pallas_call | solution.py:477
  94.4 3.5 %update_master.1 = (f32[64]{0:T(128)}, f32[304,5120]{1,0:T(8,128)}) custom-call(f32[8,128]{1,0:T(8,128)S(1)} %get-tuple-element.5.w_ref, bf16[304,128]{1,0:T(8,128)(2,1)S(1)} %copy-done.1, bf16[2,8,64,640]{3,2,1,0:T(8,128)(2,1)S(1)} %get-tuple-element.6.rt_ref, f32[304,5120]{1,0:T(8,128)S(1)} %get-tuple-element.7.master_ref), custom_call_target="tpu_custom_call" | custom-call | tf_op jit(solution)/shard_map/update_master/pallas_call | solution.py:513
Async XLA Ops:
  0.6 2.8 %copy-start = (f32[304,5120]{1,0:T(8,128)S(1)}, f32[304,5120]{1,0:T(8,128)}, u32[]{:S(2)}) copy-start(f32[304,5120]{1,0:T(8,128)} %master_ref.1) | copy-start | bytes 18677764
  3.4 0.9 copy-start.1
  4.3 0.9 copy-start.2
  5.2 0.9 copy-start.3
  6.1 0.7 copy-start.4
  6.8 0.7 copy-start.5

commit v3 on v2

--- a/solution.py
+++ b/solution.py
@@ -30,10 +30,64 @@
         return self.table.setdefault(key, len(self.table))
 
 
-SLOTS = {0: [(0, "own", 0)], 4: [(7, "up", 4)]}
+SLOTS = {0: ("own", 0), 7: ("up", 4)}
 for _s in (1, 2, 3):
-    SLOTS[_s] = [(2 * _s - 1, "up", _s), (2 * _s, "dn", _s)]
-FINE = (5, 6, 7)
+    SLOTS[2 * _s - 1], SLOTS[2 * _s] = ("up", _s), ("dn", _s)
+SLOT_OF = {where: k for k, where in SLOTS.items()}
+SND = "snd"
+RING = "z"
+LAST = "y"
+A = "A"
+B = "B"
+C = "C"
+UP = "up"
+DN = "dn"
+OPP = "opp"
+COMP = "comp"
+RIGHT_Y = "Rtr"
+RIGHT_X = "Rxr"
+RIGHT_CORE = "Rdr"
+HEAD = "head"
+A_PLANE = "A2r"
+FINE = (3, 4, 5, 6, 7)
+ORDER = (
+    (SND, LAST, B, 0, UP), (SND, LAST, B, 0, DN), (SND, RING, B, UP, 1),
+    (SND, RING, B, DN, 1), (SND, LAST, C, 0, UP), (SND, LAST, C, 0, DN),
+    (SND, RING, C, UP, 1), (SND, RING, C, DN, 1), (RIGHT_Y,), (HEAD,), (RING, B, UP, 1),
+    (SND, LAST, B, 1, UP), (SND, LAST, B, 1, DN), (SND, RING, B, UP, 2), (LAST, B, 0, UP),
+    (SND, LAST, B, 0, OPP), (LAST, C, 0, UP), (SND, LAST, C, 0, OPP), (LAST, B, 0, DN),
+    (RING, B, DN, 1), (SND, RING, B, DN, 2), (SND, LAST, B, 2, UP), (SND, LAST, B, 2, DN),
+    (LAST, C, 0, DN), (RING, C, UP, 1), (SND, LAST, C, 1, UP), (SND, LAST, C, 1, DN),
+    (SND, RING, C, UP, 2), (RING, C, DN, 1), (SND, RING, C, DN, 2), (SND, LAST, C, 2, UP),
+    (SND, LAST, C, 2, DN), (LAST, B, 1, UP), (SND, LAST, B, 1, OPP), (RING, B, UP, 2),
+    (SND, RING, B, UP, 3), (SND, LAST, B, 3, UP), (SND, LAST, B, 3, DN), (A_PLANE,),
+    (SND, RING, A, UP, 1), (SND, RING, A, DN, 1), (RING, B, DN, 2), (SND, RING, B, DN, 3),
+    (SND, LAST, B, 4, UP), (SND, LAST, B, 4, DN), (LAST, B, 1, DN), (LAST, B, 0, OPP),
+    (RING, C, UP, 2), (SND, RING, C, UP, 3), (SND, LAST, C, 3, UP), (SND, LAST, C, 3, DN),
+    (RIGHT_X,), (LAST, B, 2, UP), (SND, LAST, B, 2, OPP), (RING, C, DN, 2), (SND, RING, C, DN, 3),
+    (SND, LAST, C, 4, UP), (SND, LAST, C, 4, DN), (LAST, C, 0, OPP), (LAST, B, 2, DN),
+    (RING, B, UP, 3), (SND, RING, B, UP, 4), (SND, LAST, B, 5, UP), (SND, LAST, B, 5, DN),
+    (LAST, C, 1, UP), (SND, LAST, C, 1, OPP), (LAST, B, 1, OPP), (RIGHT_CORE,), (LAST, B, 3, UP),
+    (SND, LAST, B, 3, OPP), (RING, A, UP, 1), (SND, RING, A, UP, 2), (LAST, C, 1, DN),
+    (COMP, 0), (LAST, C, 2, UP), (SND, LAST, C, 2, OPP), (LAST, C, 2, DN), (LAST, B, 3, DN),
+    (LAST, B, 4, UP), (SND, LAST, B, 4, OPP), (RING, A, DN, 1), (SND, RING, A, DN, 2),
+    (LAST, C, 3, UP), (SND, LAST, C, 3, OPP), (LAST, B, 4, DN), (RING, B, DN, 3),
+    (SND, LAST, B, 6, UP), (SND, LAST, B, 6, DN), (LAST, C, 3, DN), (LAST, B, 2, OPP),
+    (RING, C, UP, 3), (SND, RING, C, UP, 4), (SND, LAST, C, 5, UP), (SND, LAST, C, 5, DN),
+    (LAST, C, 4, UP), (SND, LAST, C, 4, OPP), (LAST, B, 5, UP), (SND, LAST, B, 5, OPP),
+    (RING, C, DN, 3), (SND, LAST, C, 6, UP), (SND, LAST, C, 6, DN), (LAST, C, 4, DN),
+    (LAST, B, 5, DN), (RING, B, UP, 4), (SND, LAST, B, 7, UP), (SND, LAST, B, 7, DN),
+    (LAST, C, 1, OPP), (LAST, B, 3, OPP), (LAST, C, 2, OPP), (LAST, B, 4, OPP), (RING, A, UP, 2),
+    (SND, RING, A, UP, 3), (COMP, 1), (LAST, B, 6, UP), (SND, LAST, B, 6, OPP),
+    (LAST, C, 5, UP), (SND, LAST, C, 5, OPP), (LAST, C, 3, OPP), (LAST, B, 6, DN),
+    (RING, A, DN, 2), (SND, RING, A, DN, 3), (COMP, 2), (RING, C, UP, 4),
+    (SND, LAST, C, 7, UP), (SND, LAST, C, 7, DN), (LAST, C, 4, OPP), (LAST, B, 5, OPP),
+    (LAST, B, 7, UP), (SND, LAST, B, 7, OPP), (LAST, C, 5, DN), (COMP, 3), (RING, A, UP, 3),
+    (SND, RING, A, UP, 4), (LAST, C, 6, UP), (SND, LAST, C, 6, OPP), (LAST, B, 6, OPP),
+    (LAST, C, 6, DN), (LAST, B, 7, DN), (COMP, 4), (RING, A, DN, 3), (LAST, C, 7, UP),
+    (SND, LAST, C, 7, OPP), (LAST, C, 5, OPP), (LAST, B, 7, OPP), (LAST, C, 7, DN),
+    (LAST, C, 6, OPP), (RING, A, UP, 4), (COMP, 5), (LAST, C, 7, OPP), (COMP, 6), (COMP, 7),
+)
 
 
 def message_names():
@@ -82,9 +136,9 @@
 
 
 def gather_kernel(
-    hid_ref, gain_ref, right_ref, left_ref, tgt_ref, master_ref,
+    hid_in, gain_in, right_in, left_in, tgt_in, master_ref,
     out_ref, stage, rt,
-    buf_a, buf_b, buf_c, head_a, head_b, head_c, raw_a, raw_b, raw_c, sq, st, r1, r2, r3,
+    hid_ref, gain_ref, right_ref, left_ref, tgt_ref, buf_a, buf_b, buf_c, head, acc, raw_a, raw_b, raw_c, sq, st, r1, r2, r3,
     ssem, rsem, lsem,
 ):
     pop, tp = lax.axis_index("pop"), lax.axis_index("tp")
@@ -133,7 +187,8 @@
     def plane(dx, dy):
         return dev(xs[dx], ys[dy], z, c)
 
-    PLANE = [(dx, dy) for dx in range(NX) for dy in range(NY) if dx or dy]
+    far = (2, 1, 3, 0)
+    PLANE = [(dx, dy) for dx in far for dy in far if dx or dy]
 
     barrier = pltpu.get_barrier_semaphore()
     for dx, dy in PLANE:
@@ -141,8 +196,18 @@
     for device in (dev(x, y, zs[1], c), dev(x, y, zs[-1], c), sibling):
         pl.semaphore_signal(barrier, inc=1, device_id=device, device_id_type=MESH_ID)
 
-    load = pltpu.make_async_copy(master_ref, stage, lsem.at[0])
-    load.start()
+    loads = [
+        pltpu.make_async_copy(src, dst, lsem.at[i])
+        for i, (src, dst) in enumerate(
+            (
+                (hid_in, hid_ref), (gain_in, gain_ref), (right_in, right_ref),
+                (left_in, left_ref), (tgt_in, tgt_ref), (master_ref, stage),
+            )
+        )
+    ]
+    for load in loads:
+        load.start()
+    loads[0].wait()
 
     raw_a[pl.ds(x, 1)] = hid_ref[:, :WA][None]
     raw_b[pl.ds(x, 1)] = hid_ref[:, WA:WA + WB][None]
@@ -153,22 +218,23 @@
         folded = folded + piece * piece
     folded = jnp.concatenate([folded, jnp.zeros((128 - ROWS, 128), F32)], axis=0)
     row_sq = jnp.sum(folded.T, axis=0, keepdims=True)
+    loads[1].wait()
     gains = [gain_ref[pl.ds(j * 128, 128)].reshape(1, 128) for j in range(FEAT // 128)]
     packed = jnp.concatenate([row_sq] + gains + [jnp.zeros((2, 128), F32)], axis=0)
     sq[pl.ds(x, 1), pl.ds(y, 1)] = packed[None, None]
+    pl.semaphore_wait(barrier, len(PLANE) + 3)
+
+    for dx, dy in PLANE:
+        send(("sq", dx, dy), sq.at[x, y], sq.at[x, y], plane(dx, dy))
+    for d in (2, 1, 3):
+        send(("B1", d), raw_b.at[x], raw_b.at[x], plane(d, 0))
+        send(("C1", d), raw_c.at[y], raw_c.at[y], plane(0, d))
+    for d in (1, 3, 2):
+        send(("A1", d), raw_a.at[x], raw_a.at[x], plane(d, 0))
+    loads[2].wait()
     for j in range(FEAT // 128):
         block_t = right_ref[j * 128:(j + 1) * 128, :].astype(F32).T.astype(BF16)
         rt[c, pl.ds(tp, 1), :, j * 128:(j + 1) * 128] = jnp.where(c == 0, block_t[:64], block_t[64:])[None]
-
-    pl.semaphore_wait(barrier, len(PLANE) + 3)
-
-    for d in (1, 3, 2):
-        send(("B1", d), raw_b.at[x], raw_b.at[x], plane(d, 0))
-        send(("C1", d), raw_c.at[y], raw_c.at[y], plane(0, d))
-    for dx, dy in PLANE:
-        send(("sq", dx, dy), sq.at[x, y], sq.at[x, y], plane(dx, dy))
-    for d in (1, 3, 2):
-        send(("A1", d), raw_a.at[x], raw_a.at[x], plane(d, 0))
     for d in (1, 3, 2):
         send(("Rt", d), rt.at[c, tp], rt.at[c, tp], plane(0, d))
 
@@ -196,100 +262,83 @@
     def slot_z(way, s, orient=1):
         return zs[-orient * s if way == "up" else orient * s]
 
-    def last_send(part, k, zz):
-        block = z_blk(part, zz)
-        there = y_dev if part == "B" else x_dev
-        send(("last", part, k, "up"), block, block, there(1))
-        send(("last", part, k, "dn"), block, block, there(-1))
+    def hand_over(part, k, zz):
         if k in FINE:
-            send(("core", part, k, 0), block, block, sibling)
-
-    def z_start(part):
-        send(("z", part, "up", 1), z_blk(part, z), z_blk(part, z), z_dev(1))
-        send(("z", part, "dn", 1), z_blk(part, z), z_blk(part, z), z_dev(-1))
-
-    def z_recv(s, parts):
-        for part in parts:
-            for k, way, _ in SLOTS[s]:
-                zz = slot_z(way, s)
-                step = 1 if way == "up" else -1
-                recv(("z", part, way, s), z_blk(part, zz), z_dev(-step))
-                if s < (4 if way == "up" else 3):
-                    send(("z", part, way, s + 1), z_blk(part, zz), z_blk(part, zz), z_dev(step))
-                if part == "A":
-                    send(("core", "A", k), blk_a(zz), blk_a(zz), sibling)
-                else:
-                    last_send(part, k, zz)
+            send(("core", part, k, 0), z_blk(part, zz), z_blk(part, zz), sibling)
 
     def last_blk(part, zz, k):
         return blk_b(zz, yo[k]) if part == "B" else blk_c(zz, xo[k])
 
-    def y_recv(s):
-        for k, way, _ in SLOTS[s]:
-            zz = slot_z(way, s)
-            for part, there in (("B", y_dev), ("C", x_dev)):
-                below = last_blk(part, zz, -1)
-                recv(("last", part, k, "up"), below, there(-1))
-                send(("last", part, k, "opp"), below, below, there(1))
-                if k in FINE:
-                    send(("core", part, k, 1), below, below, sibling)
-
-    def o_recv(s):
-        for k, way, _ in SLOTS[s]:
-            zz = slot_z(way, s)
-            for part, ref, there in (("B", buf_b, y_dev), ("C", buf_c, x_dev)):
-                above, opposite = last_blk(part, zz, 1), last_blk(part, zz, 2)
-                recv(("last", part, k, "dn"), above, there(1))
-                if k in FINE:
-                    send(("core", part, k, 2), above, above, sibling)
-                recv(("last", part, k, "opp"), opposite, there(-1))
-                if k in FINE:
-                    send(("core", part, k, 3), opposite, opposite, sibling)
-                else:
-                    send(("core", part, k), ref.at[zz, c], ref.at[zz, c], sibling)
-
-    def core_recv(s):
-        for k, way, _ in SLOTS[s]:
-            zz = slot_z(way, s, -1)
-            recv(("core", "A", k), buf_a.at[zz, sib], sibling)
-            for part, ref, other in (("B", buf_b, yo), ("C", buf_c, xo)):
-                if k in FINE:
-                    for piece, at in ((0, 0), (1, 1), (2, -1), (3, 2)):
-                        recv(("core", part, k, piece), ref.at[zz, sib, other[at]], sibling)
-                else:
-                    recv(("core", part, k), ref.at[zz, sib], sibling)
+    def ring_send(part, way, s):
+        block = z_blk(part, slot_z(way, s - 1))
+        send(("z", part, way, s), block, block, z_dev(1 if way == "up" else -1))
+
+    def last_send(part, k, way):
+        zz = slot_z(*SLOTS[k])
+        block = last_blk(part, zz, -1 if way == "opp" else 0)
+        there = y_dev if part == "B" else x_dev
+        send(("last", part, k, way), block, block, there(-1 if way == "dn" else 1))
+
+    def take_z(part, way, s):
+        k = SLOT_OF[way, s]
+        zz = slot_z(way, s)
+        block = z_blk(part, zz)
+        recv(("z", part, way, s), block, z_dev(-1 if way == "up" else 1))
+        if part == "A":
+            send(("core", "A", k), block, block, sibling)
+        else:
+            hand_over(part, k, zz)
+
+    pieces_in = {}
+
+    def take_last(part, k, way):
+        zz = slot_z(*SLOTS[k])
+        there = y_dev if part == "B" else x_dev
+        block = last_blk(part, zz, {"up": -1, "dn": 1, "opp": 2}[way])
+        recv(("last", part, k, way), block, there(1 if way == "dn" else -1))
+        if k in FINE:
+            send(("core", part, k, {"up": 1, "dn": 2, "opp": 3}[way]), block, block, sibling)
+        else:
+            pieces_in[part, k] = pieces_in.get((part, k), 0) + 1
+            if pieces_in[part, k] == 3:
+                whole = (buf_b if part == "B" else buf_c).at[zz, c]
+                send(("core", part, k), whole, whole, sibling)
+
+    def core_recv(k, zz):
+        recv(("core", "A", k), buf_a.at[zz, sib], sibling)
+        for part, ref, other in (("B", buf_b, yo), ("C", buf_c, xo)):
+            if k in FINE:
+                for piece, at in ((0, 0), (1, 1), (2, -1), (3, 2)):
+                    recv(("core", part, k, piece), ref.at[zz, sib, other[at]], sibling)
+            else:
+                recv(("core", part, k), ref.at[zz, sib], sibling)
 
     def fill_head(lo, hi, source):
         for t in range(8):
             hi_t, y_t = divmod(t, NY)
-            j = y_t * 2 + hi_t
             tile = source(t)
-            head_a[lo:hi, j * WA:(j + 1) * WA] = tile[:, :WA]
-            head_b[lo:hi, j * WB:(j + 1) * WB] = tile[:, WA:WA + WB]
-            head_c[lo:hi, j * WB:(j + 1) * WB] = tile[:, WA + WB:]
+            head[y_t, lo:hi, hi_t * WA:(hi_t + 1) * WA] = tile[:, :WA]
+            head[y_t, lo:hi, 2 * WA + hi_t * WB:2 * WA + (hi_t + 1) * WB] = tile[:, WA:WA + WB]
+            head[y_t, lo:hi, 2 * (WA + WB) + hi_t * WB:2 * (WA + WB) + (hi_t + 1) * WB] = tile[:, WA + WB:]
 
     offset = (pop * 8 + tp) * VOC
 
     def compute_one(zz):
-        def tokens(piece):
-            return jnp.concatenate(
-                [
-                    jnp.concatenate([piece(cc, yy, hi * 2 + lo) for lo in range(2) for cc in range(2)], axis=0)
-                    for yy in range(NY)
-                    for hi in range(2)
-                ],
-                axis=1,
+        def tokens(piece, hi):
+            return jnp.concatenate([piece(cc, hi * 2 + lo) for lo in range(2) for cc in range(2)], axis=0)
+
+        def features(yy, carry):
+            columns = [tokens(lambda cc, xx: buf_a[zz, cc, yy, xx], hi) for hi in range(2)]
+            columns += [tokens(lambda cc, xx: buf_b[zz, cc, yy, xx], hi) for hi in range(2)]
+            columns += [tokens(lambda cc, xx: buf_c[zz, cc, xx, yy], hi) for hi in range(2)]
+            acc[...] += lax.dot_general(
+                head[yy], jnp.concatenate(columns, axis=1), NT, preferred_element_type=F32
             )
-
-        full = lax.dot_general(
-            head_b[...], tokens(lambda cc, yy, xx: buf_b[zz, cc, yy, xx]), NT, preferred_element_type=F32
-        )
-        full += lax.dot_general(
-            head_c[...], tokens(lambda cc, yy, xx: buf_c[zz, cc, xx, yy]), NT, preferred_element_type=F32
-        )
-        full += lax.dot_general(
-            head_a[...], tokens(lambda cc, yy, xx: buf_a[zz, cc, yy, xx]), NT, preferred_element_type=F32
-        )
+            return carry
+
+        acc[...] = jnp.zeros((AUG, 256), F32)
+        lax.fori_loop(0, NY, features, 0)
+        full = acc[...]
         lane = lax.broadcasted_iota(jnp.int32, (FACT, 256), 1)
         column = lax.broadcasted_iota(jnp.int32, (FACT, 256), 0)
         lane_lo = lax.shift_right_logical(lane, 7)
@@ -312,22 +361,53 @@
     def stat_send(k):
         for i in range(2):
             if i or k:
-                send(("stat1", i, k % 8), st.at[zs[k], los[i]], r1.at[blk], dev(x_hi * 2 + los[i], y, zs[k], c))
-
-    def compute(s):
-        core_recv(s)
-
-        def loop(i, carry):
-            compute_one(lax.rem(z + (2 * i - 1) * s + NZ, NZ))
-            return carry
-
-        if s in (0, 4):
-            compute_one(zs[s])
+                send(("stat1", i, k), st.at[zs[(k + 4) % 8], los[i]], r1.at[blk], dev(x_hi * 2 + los[i], y, zs[k], c))
+
+    def compute(k):
+        way, s = SLOTS[k]
+        zz = slot_z(way, s, -1)
+        core_recv(k, zz)
+        compute_one(zz)
+        stat_send(((8 - s if way == "dn" else s) + 4) % 8)
+
+    def step(what, *which):
+        if what == "snd":
+            (ring_send if which[0] == "z" else last_send)(*which[1:])
+        elif what == "z":
+            take_z(*which)
+        elif what == "y":
+            take_last(*which)
+        elif what == "comp":
+            compute(*which)
+        elif what == "head":
+            for load in loads[3:]:
+                load.wait()
+            fill_head(0, VOC, lambda t: stage[:, t * FEAT:(t + 1) * FEAT].astype(BF16))
+        elif what == "A2r":
+            for d in (1, 3, 2):
+                recv(("A2", d), buf_a.at[z, c, ys[-d]], plane(0, -d))
+            send(("core", "A", 0), blk_a(z), blk_a(z), sibling)
+        elif what == "Rtr":
+            for d in range(1, 4):
+                recv(("Rt", d), rt.at[c, x_hi * NY + ys[-d]], plane(0, -d))
+            send(("Rx",), rt.at[c, pl.ds(x_hi * NY, NY)], rt.at[c, pl.ds(x_hi * NY, NY)], mirror)
+        elif what == "Rxr":
+            recv(("Rx",), rt.at[c, pl.ds((1 - x_hi) * NY, NY)], mirror)
+            send(("Rd",), rt.at[c], rt.at[c], sibling)
         else:
-            lax.fori_loop(0, 2, loop, 0)
-        stat_send(s)
-        if s in (1, 2, 3):
-            stat_send(8 - s)
+            recv(("Rd",), rt.at[sib], sibling)
+            fill_head(VOC, VOC + 64, lambda t: rt[0, t])
+            fill_head(VOC + 64, AUG, lambda t: rt[1, t])
+
+    def follow(first, part):
+        at = first
+        while at < len(ORDER):
+            action = ORDER[at]
+            if part is not None and not (action[0] == "snd" and action[2] == part):
+                break
+            step(*action)
+            at += 1
+        return at
 
     for dx, dy in PLANE:
         recv(("sq", dx, dy), sq.at[xs[-dx], ys[-dy]], plane(-dx, -dy))
@@ -351,61 +431,24 @@
         recv(("B1", d), raw_b.at[xs[-d]], plane(-d, 0))
     for t in range(NX):
         buf_b[z, c, y, t] = normalize(raw_b[t], scales[t % 2], t, y, 1, 2)
-    z_start("B")
-    last_send("B", 0, z)
+    hand_over("B", 0, z)
+    start_from = follow(0, "B")
     for d in (1, 3, 2):
         recv(("C1", d), raw_c.at[ys[-d]], plane(0, -d))
     for t in range(NY):
         buf_c[z, c, x, t] = normalize(raw_c[t], own_scale, x, t, 3, 2)
-    z_start("C")
-    last_send("C", 0, z)
+    hand_over("C", 0, z)
+    start_from = follow(start_from, "C")
     for d in (1, 3, 2):
         recv(("A1", d), raw_a.at[xs[-d]], plane(-d, 0))
     for t in range(NX):
         buf_a[z, c, y, t] = normalize(raw_a[t], scales[t % 2], t, y, 0, 1)
     for d in (1, 3, 2):
         send(("A2", d), buf_a.at[z, c, y], buf_a.at[z, c, y], plane(0, d))
-    for d in range(1, 4):
-        recv(("Rt", d), rt.at[c, x_hi * NY + ys[-d]], plane(0, -d))
-    send(("Rx",), rt.at[c, pl.ds(x_hi * NY, NY)], rt.at[c, pl.ds(x_hi * NY, NY)], mirror)
-
-    load.wait()
-    fill_head(0, VOC, lambda t: stage[:, t * FEAT:(t + 1) * FEAT].astype(BF16))
-
-    z_recv(1, "BC")
-    y_recv(0)
-    z_recv(2, "BC")
-    for d in (1, 3, 2):
-        recv(("A2", d), buf_a.at[z, c, ys[-d]], plane(0, -d))
-    z_start("A")
-    send(("core", "A", 0), blk_a(z), blk_a(z), sibling)
-    recv(("Rx",), rt.at[c, pl.ds((1 - x_hi) * NY, NY)], mirror)
-    send(("Rd",), rt.at[c], rt.at[c], sibling)
-    y_recv(1)
-    o_recv(0)
-    z_recv(3, "BC")
-    z_recv(1, "A")
-    y_recv(2)
-    o_recv(1)
-    recv(("Rd",), rt.at[sib], sibling)
-    fill_head(VOC, VOC + 64, lambda t: rt[0, t])
-    fill_head(VOC + 64, AUG, lambda t: rt[1, t])
-    compute(0)
-    z_recv(4, "BC")
-    z_recv(2, "A")
-    compute(1)
-    y_recv(3)
-    o_recv(2)
-    z_recv(3, "A")
-    compute(2)
-    y_recv(4)
-    o_recv(3)
-    z_recv(4, "A")
-    o_recv(4)
-    compute(3)
-    compute(4)
-
-    r1[pl.ds(blk, 1)] = st[z, x_lo][None]
+
+    follow(start_from, None)
+
+    r1[pl.ds(blk, 1)] = st[zs[4], x_lo][None]
     for copy in sent:
         copy.wait_send()
     sent.clear()
@@ -423,7 +466,8 @@
         cc = c if i == 0 else sib
         return cc, hi, d
 
-    QUAD = [(i, k) for i in range(2) for k in range(8) if i or k]
+    QUAD = [(i, k) for i in (1, 0) for k in (6, 2, 5, 7, 1, 3, 4, 0) if i or k]
+    RING = [(i, k) for i in (1, 0) for k in (4, 3, 5, 2, 6, 1, 7, 0) if i or k]
     for i, k in QUAD:
         cc, hi, d = quad_at(i, k)
         send(("stat2", i, k), r2.at[quad], r2.at[quad], dev(hi * 2 + x_lo, ys[d], z, cc))
@@ -439,15 +483,16 @@
         for m in range(4)
     ]
     loglik, weights = zero, zero
+    owned = x_lo * NZ + zs[4]
     for m in range(4):
-        loglik = jnp.where(lane == blk * 4 + m, means[m], loglik)
+        loglik = jnp.where(lane == owned * 4 + m, means[m], loglik)
     for h in range(2):
-        weights = jnp.where(lax.shift_right_logical(lane, 2) == blk * 2 + h, means[2 * h] - means[2 * h + 1], weights)
+        weights = jnp.where(lax.shift_right_logical(lane, 2) == owned * 2 + h, means[2 * h] - means[2 * h + 1], weights)
     packed = jnp.concatenate([loglik, weights, jnp.zeros((6, 128), F32)], axis=0)
     r3[pl.ds(blk, 1)] = packed[None]
-    for i, k in QUAD:
+    for i, k in RING:
         send(("stat3", i, k), r3.at[blk], r3.at[blk], dev(x_hi * 2 + los[i], y, zs[k], c))
-    for i, k in QUAD:
+    for i, k in RING:
         zz = zs[-k if k < 5 else 8 - k]
         recv(("stat3", i, k), r3.at[los[i] * NZ + zz], dev(x_hi * 2 + los[i], y, zz, c))
     out_ref[...] = jnp.sum(r3[...], axis=0)
@@ -481,15 +526,19 @@
             pltpu.VMEM((VOC, D), F32),
             pltpu.VMEM((2, 8, 64, FEAT), BF16),
         ),
-        in_specs=[vmem, vmem, vmem, vmem, vmem, hbm],
+        in_specs=[hbm] * 6,
         out_specs=(vmem, vmem, vmem),
         scratch_shapes=[
+            pltpu.VMEM((ROWS, FEAT), BF16),
+            pltpu.VMEM((FEAT,), F32),
+            pltpu.VMEM((FEAT, FACT), BF16),
+            pltpu.VMEM((VOC, FACT), BF16),
+            pltpu.VMEM((16, 1, 128), jnp.int32),
             pltpu.VMEM((NZ, 2, NY, NX, ROWS, WA), BF16),
             pltpu.VMEM((NZ, 2, NY, NX, ROWS, WB), BF16),
             pltpu.VMEM((NZ, 2, NX, NY, ROWS, WB), BF16),
-            pltpu.VMEM((AUG, 8 * WA), BF16),
-            pltpu.VMEM((AUG, 8 * WB), BF16),
-            pltpu.VMEM((AUG, 8 * WB), BF16),
+            pltpu.VMEM((NY, AUG, 2 * FEAT), BF16),
+            pltpu.VMEM((AUG, 256), F32),
             pltpu.VMEM((NX, ROWS, WA), BF16),
             pltpu.VMEM((NX, ROWS, WB), BF16),
             pltpu.VMEM((NY, ROWS, WB), BF16),
@@ -500,10 +549,10 @@
             pltpu.VMEM((16, 8, 128), F32),
             pltpu.SemaphoreType.DMA((N_MSG,)),
             pltpu.SemaphoreType.DMA((N_MSG,)),
-            pltpu.SemaphoreType.DMA((1,)),
+            pltpu.SemaphoreType.DMA((6,)),
         ],
         compiler_params=pltpu.CompilerParams(
-            collective_id=0, has_side_effects=True, vmem_limit_bytes=40 * 1024 * 1024
+            collective_id=0, has_side_effects=True, vmem_limit_bytes=52 * 1024 * 1024
         ),
         name="gather_logits",
     )(

time: 98.2 us -> 86.4 us (0.88)
  local copies, waits for them, and re-layouts: 6.83 us -> 0.01 us
  Pallas kernels: 90.4 us -> 85.7 us
    unnamed x12 -> x2, local copies, waits for them, and re-layouts: 6.83 us -> 0.01 us
    pallas_call x1, Pallas kernels: 86.9 us -> 82.1 us  [body(): pl.pallas_call(gather_kernel, out_shape=(pltpu.VMEM((8, 128), F32), pltpu...]
where the time goes in v3:
time: 86.4 us; the launch traced here: 86.3 us
  Pallas kernels  85.7 us (99%)
    pallas_call x1, Pallas kernels, body(): pl.pallas_call(gather_kernel, out_shape=(pltpu.VMEM((8, 128), F32), pltpu...  82.1 us
    pallas_call x1, Pallas kernels, body(): pl.pallas_call(update_kernel, out_shape=(jax.ShapeDtypeStruct((64,), F32)...  3.54 us

profile of v3, /device:TPU:1, one launch (start us, length us, event | category | flops | bytes accessed | tf_op | source)
XLA Modules:
  0.0 86.3 jit_solution(14651945601036193051)
XLA Ops:
  0.6 0.0 copy-start
  0.6 82.1 %gather_logits.1 = (f32[8,128]{1,0:T(8,128)S(1)}, f32[304,5120]{1,0:T(8,128)S(1)}, bf16[2,8,64,640]{3,2,1,0:T(8,128)(2,1)S(1)}) custom-call(bf16[64,640]{1,0:T(8,128)(2,1)} %hid_in.1, f32[640]{0:T(1024)} %gain_in.1, bf16[640,128]{1,0:T(8,128)(2,1)} %right_in.1, bf16[304,128]{1,0:T(8,128)(2,1)} %left_ref.1, s32[16,1,128]{2,1,0:T(1,128)} %bitcast.1, ...), custom_call_target="tpu_custom_call" | custom-call | tf_op jit(solution)/shard_map/gather_logits/pallas_call | solution.py:522
  82.8 0.0 copy-done
  82.8 3.5 %update_master.1 = (f32[64]{0:T(128)}, f32[304,5120]{1,0:T(8,128)}) custom-call(f32[8,128]{1,0:T(8,128)S(1)} %get-tuple-element.5.w_ref, bf16[304,128]{1,0:T(8,128)(2,1)S(1)} %copy-done, bf16[2,8,64,640]{3,2,1,0:T(8,128)(2,1)S(1)} %get-tuple-element.6.rt_ref, f32[304,5120]{1,0:T(8,128)S(1)} %get-tuple-element.7.master_ref), custom_call_target="tpu_custom_call" | custom-call | tf_op jit(solution)/shard_map/update_master/pallas_call | solution.py:562
Async XLA Ops:
  0.6 82.2 %copy-start = (bf16[304,128]{1,0:T(8,128)(2,1)S(1)}, bf16[304,128]{1,0:T(8,128)(2,1)}, u32[]{:S(2)}) copy-start(bf16[304,128]{1,0:T(8,128)(2,1)} %left_ref.1) | copy-start | bytes 233476

commit v4 on v3

--- a/solution.py
+++ b/solution.py
@@ -16,7 +16,6 @@
 WA, WB = 128, 256
 VOC = 304
 FACT = 128
-AUG = VOC + FACT
 F32, BF16 = jnp.float32, jnp.bfloat16
 MESH_ID = pl.DeviceIdType.MESH
 NT = (((1,), (1,)), ((), ()))
@@ -68,7 +67,7 @@
     (SND, LAST, C, 4, UP), (SND, LAST, C, 4, DN), (LAST, C, 0, OPP), (LAST, B, 2, DN),
     (RING, B, UP, 3), (SND, RING, B, UP, 4), (SND, LAST, B, 5, UP), (SND, LAST, B, 5, DN),
     (LAST, C, 1, UP), (SND, LAST, C, 1, OPP), (LAST, B, 1, OPP), (RIGHT_CORE,), (LAST, B, 3, UP),
-    (SND, LAST, B, 3, OPP), (RING, A, UP, 1), (SND, RING, A, UP, 2), (LAST, C, 1, DN),
+    (SND, LAST, B, 3, OPP), (LAST, C, 1, DN), (RING, A, UP, 1), (SND, RING, A, UP, 2),
     (COMP, 0), (LAST, C, 2, UP), (SND, LAST, C, 2, OPP), (LAST, C, 2, DN), (LAST, B, 3, DN),
     (LAST, B, 4, UP), (SND, LAST, B, 4, OPP), (RING, A, DN, 1), (SND, RING, A, DN, 2),
     (LAST, C, 3, UP), (SND, LAST, C, 3, OPP), (LAST, B, 4, DN), (RING, B, DN, 3),
@@ -82,11 +81,12 @@
     (LAST, C, 5, UP), (SND, LAST, C, 5, OPP), (LAST, C, 3, OPP), (LAST, B, 6, DN),
     (RING, A, DN, 2), (SND, RING, A, DN, 3), (COMP, 2), (RING, C, UP, 4),
     (SND, LAST, C, 7, UP), (SND, LAST, C, 7, DN), (LAST, C, 4, OPP), (LAST, B, 5, OPP),
-    (LAST, B, 7, UP), (SND, LAST, B, 7, OPP), (LAST, C, 5, DN), (COMP, 3), (RING, A, UP, 3),
-    (SND, RING, A, UP, 4), (LAST, C, 6, UP), (SND, LAST, C, 6, OPP), (LAST, B, 6, OPP),
-    (LAST, C, 6, DN), (LAST, B, 7, DN), (COMP, 4), (RING, A, DN, 3), (LAST, C, 7, UP),
-    (SND, LAST, C, 7, OPP), (LAST, C, 5, OPP), (LAST, B, 7, OPP), (LAST, C, 7, DN),
-    (LAST, C, 6, OPP), (RING, A, UP, 4), (COMP, 5), (LAST, C, 7, OPP), (COMP, 6), (COMP, 7),
+    (LAST, B, 7, UP), (SND, LAST, B, 7, OPP), (LAST, C, 5, DN), (COMP, 3), (LAST, C, 6, UP),
+    (SND, LAST, C, 6, OPP), (LAST, C, 6, DN), (LAST, B, 7, DN), (LAST, B, 6, OPP),
+    (RING, A, UP, 3), (SND, RING, A, UP, 4), (COMP, 4), (LAST, C, 7, UP),
+    (SND, LAST, C, 7, OPP), (LAST, C, 5, OPP), (LAST, B, 7, OPP), (RING, A, DN, 3),
+    (LAST, C, 7, DN), (LAST, C, 6, OPP), (COMP, 5), (LAST, C, 7, OPP), (RING, A, UP, 4),
+    (COMP, 6), (COMP, 7),
 )
 
 
@@ -138,7 +138,7 @@
 def gather_kernel(
     hid_in, gain_in, right_in, left_in, tgt_in, master_ref,
     out_ref, stage, rt,
-    hid_ref, gain_ref, right_ref, left_ref, tgt_ref, buf_a, buf_b, buf_c, head, acc, raw_a, raw_b, raw_c, sq, st, r1, r2, r3,
+    hid_ref, gain_ref, right_ref, left_ref, tgt_ref, buf_a, buf_b, buf_c, head, slot_right, acc, raw_a, raw_b, raw_c, sq, st, r1, r2, r3,
     ssem, rsem, lsem,
 ):
     pop, tp = lax.axis_index("pop"), lax.axis_index("tp")
@@ -313,13 +313,27 @@
             else:
                 recv(("core", part, k), ref.at[zz, sib], sibling)
 
-    def fill_head(lo, hi, source):
+    def by_part(t):
+        hi_t = t // NY
+        yield slice(0, WA), slice(hi_t * WA, (hi_t + 1) * WA)
+        for i in range(2):
+            start = 2 * WA + (2 * i + hi_t) * WB
+            yield slice(WA + i * WB, WA + (i + 1) * WB), slice(start, start + WB)
+
+    def fill_head():
         for t in range(8):
-            hi_t, y_t = divmod(t, NY)
-            tile = source(t)
-            head[y_t, lo:hi, hi_t * WA:(hi_t + 1) * WA] = tile[:, :WA]
-            head[y_t, lo:hi, 2 * WA + hi_t * WB:2 * WA + (hi_t + 1) * WB] = tile[:, WA:WA + WB]
-            head[y_t, lo:hi, 2 * (WA + WB) + hi_t * WB:2 * (WA + WB) + (hi_t + 1) * WB] = tile[:, WA + WB:]
+            for source, place in by_part(t):
+                columns = slice(t * FEAT + source.start, t * FEAT + source.stop)
+                head[t % NY, :, place] = stage[:, columns].astype(BF16)
+
+    def fill_right():
+        for t in range(8):
+            halves = [rt[half, t].astype(F32) for half in range(2)]
+            for zz in range(NZ):
+                rows = slice(8 * zz, 8 * zz + 8)
+                both = jnp.concatenate([half[rows] for half in halves], axis=0).astype(BF16)
+                for source, place in by_part(t):
+                    slot_right[zz, t % NY, :, place] = both[:, source]
 
     offset = (pop * 8 + tp) * VOC
 
@@ -332,22 +346,24 @@
             columns += [tokens(lambda cc, xx: buf_b[zz, cc, yy, xx], hi) for hi in range(2)]
             columns += [tokens(lambda cc, xx: buf_c[zz, cc, xx, yy], hi) for hi in range(2)]
             acc[...] += lax.dot_general(
-                head[yy], jnp.concatenate(columns, axis=1), NT, preferred_element_type=F32
+                jnp.concatenate([head[yy], slot_right[zz, yy]], axis=0),
+                jnp.concatenate(columns, axis=1), NT, preferred_element_type=F32,
             )
             return carry
 
-        acc[...] = jnp.zeros((AUG, 256), F32)
+        acc[...] = jnp.zeros((VOC + 16, 256), F32)
         lax.fori_loop(0, NY, features, 0)
         full = acc[...]
-        lane = lax.broadcasted_iota(jnp.int32, (FACT, 256), 1)
-        column = lax.broadcasted_iota(jnp.int32, (FACT, 256), 0)
-        lane_lo = lax.shift_right_logical(lane, 7)
-        lane_c = lax.bitwise_and(lax.shift_right_logical(lane, 6), 1)
-        pair = (lane_lo * NZ + zz) * 2 + lane_c
+        lane = lax.broadcasted_iota(jnp.int32, (16, 256), 1)
+        column = lax.broadcasted_iota(jnp.int32, (16, 256), 0)
+        own = lax.shift_right_logical(column, 2) == lax.shift_right_logical(lane, 6)
         odd = lax.bitwise_and(lax.shift_right_logical(lane, 5), 1)
-        own = lax.shift_right_logical(column, 2) == pair
         sign = jnp.where(odd == 0, SIGMA_NOISE, -SIGMA_NOISE)
-        lowrank = jnp.where(own, full[VOC:] * sign, 0.0).astype(BF16)
+        few = jnp.where(own, full[VOC:] * sign, 0.0)
+        spread = jnp.concatenate([few[:8]] * NZ + [few[8:]] * NZ, axis=0)
+        place = lax.broadcasted_iota(jnp.int32, (FACT, 256), 0)
+        here = lax.bitwise_and(lax.shift_right_logical(place, 3), NZ - 1) == zz
+        lowrank = jnp.where(here, spread, 0.0).astype(BF16)
         logits = full[:VOC] + jnp.dot(left_ref[...], lowrank, preferred_element_type=F32)
         best = jnp.max(logits, axis=0, keepdims=True)
         total = jnp.sum(jnp.exp(logits - best), axis=0, keepdims=True)
@@ -382,7 +398,7 @@
         elif what == "head":
             for load in loads[3:]:
                 load.wait()
-            fill_head(0, VOC, lambda t: stage[:, t * FEAT:(t + 1) * FEAT].astype(BF16))
+            fill_head()
         elif what == "A2r":
             for d in (1, 3, 2):
                 recv(("A2", d), buf_a.at[z, c, ys[-d]], plane(0, -d))
@@ -396,8 +412,7 @@
             send(("Rd",), rt.at[c], rt.at[c], sibling)
         else:
             recv(("Rd",), rt.at[sib], sibling)
-            fill_head(VOC, VOC + 64, lambda t: rt[0, t])
-            fill_head(VOC + 64, AUG, lambda t: rt[1, t])
+            fill_right()
 
     def follow(first, part):
         at = first
@@ -537,8 +552,9 @@
             pltpu.VMEM((NZ, 2, NY, NX, ROWS, WA), BF16),
             pltpu.VMEM((NZ, 2, NY, NX, ROWS, WB), BF16),
             pltpu.VMEM((NZ, 2, NX, NY, ROWS, WB), BF16),
-            pltpu.VMEM((NY, AUG, 2 * FEAT), BF16),
-            pltpu.VMEM((AUG, 256), F32),
+            pltpu.VMEM((NY, VOC, 2 * FEAT), BF16),
+            pltpu.VMEM((NZ, NY, 16, 2 * FEAT), BF16),
+            pltpu.VMEM((VOC + 16, 256), F32),
             pltpu.VMEM((NX, ROWS, WA), BF16),
             pltpu.VMEM((NX, ROWS, WB), BF16),
             pltpu.VMEM((NY, ROWS, WB), BF16),

time: 86.4 us -> 84.3 us (0.976)
  Pallas kernels: 85.7 us -> 83.4 us
    pallas_call x1, Pallas kernels: 82.1 us -> 79.8 us  [body(): pl.pallas_call(gather_kernel, out_shape=(pltpu.VMEM((8, 128), F32), pltpu...]
where the time goes in v4:
time: 84.3 us; the launch traced here: 84 us
  Pallas kernels  83.4 us (99%)
    pallas_call x1, Pallas kernels, body(): pl.pallas_call(gather_kernel, out_shape=(pltpu.VMEM((8, 128), F32), pltpu...  79.8 us
    pallas_call x1, Pallas kernels, body(): pl.pallas_call(update_kernel, out_shape=(jax.ShapeDtypeStruct((64,), F32)...  3.54 us

profile of v4, /device:TPU:1, one launch (start us, length us, event | category | flops | bytes accessed | tf_op | source)
XLA Modules:
  0.0 84.0 jit_solution(5290403581410963625)
XLA Ops:
  0.6 0.0 copy-start
  0.6 79.8 %gather_logits.1 = (f32[8,128]{1,0:T(8,128)S(1)}, f32[304,5120]{1,0:T(8,128)S(1)}, bf16[2,8,64,640]{3,2,1,0:T(8,128)(2,1)S(1)}) custom-call(bf16[64,640]{1,0:T(8,128)(2,1)} %hid_in.1, f32[640]{0:T(1024)} %gain_in.1, bf16[640,128]{1,0:T(8,128)(2,1)} %right_in.1, bf16[304,128]{1,0:T(8,128)(2,1)} %left_ref.1, s32[16,1,128]{2,1,0:T(1,128)} %bitcast.1, ...), custom_call_target="tpu_custom_call" | custom-call | tf_op jit(solution)/shard_map/gather_logits/pallas_call | solution.py:537
  80.5 0.0 copy-done
  80.5 3.5 %update_master.1 = (f32[64]{0:T(128)}, f32[304,5120]{1,0:T(8,128)}) custom-call(f32[8,128]{1,0:T(8,128)S(1)} %get-tuple-element.5.w_ref, bf16[304,128]{1,0:T(8,128)(2,1)S(1)} %copy-done, bf16[2,8,64,640]{3,2,1,0:T(8,128)(2,1)S(1)} %get-tuple-element.6.rt_ref, f32[304,5120]{1,0:T(8,128)S(1)} %get-tuple-element.7.master_ref), custom_call_target="tpu_custom_call" | custom-call | tf_op jit(solution)/shard_map/update_master/pallas_call | solution.py:578
Async XLA Ops:
  0.6 79.8 %copy-start = (bf16[304,128]{1,0:T(8,128)(2,1)S(1)}, bf16[304,128]{1,0:T(8,128)(2,1)}, u32[]{:S(2)}) copy-start(bf16[304,128]{1,0:T(8,128)(2,1)} %left_ref.1) | copy-start | bytes 233476

commit v5 on v4

--- a/solution.py
+++ b/solution.py
@@ -68,7 +68,7 @@
     (RING, B, UP, 3), (SND, RING, B, UP, 4), (SND, LAST, B, 5, UP), (SND, LAST, B, 5, DN),
     (LAST, C, 1, UP), (SND, LAST, C, 1, OPP), (LAST, B, 1, OPP), (RIGHT_CORE,), (LAST, B, 3, UP),
     (SND, LAST, B, 3, OPP), (LAST, C, 1, DN), (RING, A, UP, 1), (SND, RING, A, UP, 2),
-    (COMP, 0), (LAST, C, 2, UP), (SND, LAST, C, 2, OPP), (LAST, C, 2, DN), (LAST, B, 3, DN),
+    (COMP, 0), (LAST, C, 2, UP), (SND, LAST, C, 2, OPP), (LAST, B, 3, DN), (LAST, C, 2, DN),
     (LAST, B, 4, UP), (SND, LAST, B, 4, OPP), (RING, A, DN, 1), (SND, RING, A, DN, 2),
     (LAST, C, 3, UP), (SND, LAST, C, 3, OPP), (LAST, B, 4, DN), (RING, B, DN, 3),
     (SND, LAST, B, 6, UP), (SND, LAST, B, 6, DN), (LAST, C, 3, DN), (LAST, B, 2, OPP),
@@ -78,15 +78,14 @@
     (LAST, B, 5, DN), (RING, B, UP, 4), (SND, LAST, B, 7, UP), (SND, LAST, B, 7, DN),
     (LAST, C, 1, OPP), (LAST, B, 3, OPP), (LAST, C, 2, OPP), (LAST, B, 4, OPP), (RING, A, UP, 2),
     (SND, RING, A, UP, 3), (COMP, 1), (LAST, B, 6, UP), (SND, LAST, B, 6, OPP),
-    (LAST, C, 5, UP), (SND, LAST, C, 5, OPP), (LAST, C, 3, OPP), (LAST, B, 6, DN),
-    (RING, A, DN, 2), (SND, RING, A, DN, 3), (COMP, 2), (RING, C, UP, 4),
-    (SND, LAST, C, 7, UP), (SND, LAST, C, 7, DN), (LAST, C, 4, OPP), (LAST, B, 5, OPP),
-    (LAST, B, 7, UP), (SND, LAST, B, 7, OPP), (LAST, C, 5, DN), (COMP, 3), (LAST, C, 6, UP),
-    (SND, LAST, C, 6, OPP), (LAST, C, 6, DN), (LAST, B, 7, DN), (LAST, B, 6, OPP),
-    (RING, A, UP, 3), (SND, RING, A, UP, 4), (COMP, 4), (LAST, C, 7, UP),
-    (SND, LAST, C, 7, OPP), (LAST, C, 5, OPP), (LAST, B, 7, OPP), (RING, A, DN, 3),
-    (LAST, C, 7, DN), (LAST, C, 6, OPP), (COMP, 5), (LAST, C, 7, OPP), (RING, A, UP, 4),
-    (COMP, 6), (COMP, 7),
+    (LAST, C, 3, OPP), (LAST, C, 5, UP), (SND, LAST, C, 5, OPP), (COMP, 2), (LAST, B, 6, DN),
+    (LAST, C, 5, DN), (RING, A, DN, 2), (SND, RING, A, DN, 3), (LAST, B, 5, OPP),
+    (RING, C, UP, 4), (SND, LAST, C, 7, UP), (SND, LAST, C, 7, DN), (LAST, C, 4, OPP),
+    (COMP, 3), (LAST, C, 6, UP), (SND, LAST, C, 6, OPP), (LAST, B, 7, UP),
+    (SND, LAST, B, 7, OPP), (LAST, B, 7, DN), (COMP, 4), (LAST, B, 6, OPP), (LAST, C, 6, DN),
+    (RING, A, UP, 3), (SND, RING, A, UP, 4), (LAST, C, 5, OPP), (RING, A, DN, 3),
+    (LAST, C, 7, UP), (SND, LAST, C, 7, OPP), (LAST, B, 7, OPP), (LAST, C, 7, DN),
+    (LAST, C, 6, OPP), (COMP, 5), (LAST, C, 7, OPP), (RING, A, UP, 4), (COMP, 6), (COMP, 7),
 )
 
 

time: 84.3 us -> 84.4 us (level)
  no operation moved by 1% of the time
where the time goes in v5:
time: 84.4 us; the launch traced here: 84.3 us
  Pallas kernels  83.6 us (99%)
    pallas_call x1, Pallas kernels, body(): pl.pallas_call(gather_kernel, out_shape=(pltpu.VMEM((8, 128), F32), pltpu...  80.1 us
    pallas_call x1, Pallas kernels, body(): pl.pallas_call(update_kernel, out_shape=(jax.ShapeDtypeStruct((64,), F32)...  3.54 us

profile of v5, /device:TPU:1, one launch (start us, length us, event | category | flops | bytes accessed | tf_op | source)
XLA Modules:
  0.0 84.3 jit_solution(6878317734676220039)
XLA Ops:
  0.6 0.0 copy-start
  0.6 80.1 %gather_logits.1 = (f32[8,128]{1,0:T(8,128)S(1)}, f32[304,5120]{1,0:T(8,128)S(1)}, bf16[2,8,64,640]{3,2,1,0:T(8,128)(2,1)S(1)}) custom-call(bf16[64,640]{1,0:T(8,128)(2,1)} %hid_in.1, f32[640]{0:T(1024)} %gain_in.1, bf16[640,128]{1,0:T(8,128)(2,1)} %right_in.1, bf16[304,128]{1,0:T(8,128)(2,1)} %left_ref.1, s32[16,1,128]{2,1,0:T(1,128)} %bitcast.1, ...), custom_call_target="tpu_custom_call" | custom-call | tf_op jit(solution)/shard_map/gather_logits/pallas_call | solution.py:536
  80.8 0.0 copy-done
  80.8 3.5 %update_master.1 = (f32[64]{0:T(128)}, f32[304,5120]{1,0:T(8,128)}) custom-call(f32[8,128]{1,0:T(8,128)S(1)} %get-tuple-element.5.w_ref, bf16[304,128]{1,0:T(8,128)(2,1)S(1)} %copy-done, bf16[2,8,64,640]{3,2,1,0:T(8,128)(2,1)S(1)} %get-tuple-element.6.rt_ref, f32[304,5120]{1,0:T(8,128)S(1)} %get-tuple-element.7.master_ref), custom_call_target="tpu_custom_call" | custom-call | tf_op jit(solution)/shard_map/update_master/pallas_call | solution.py:577
Async XLA Ops:
  0.6 80.1 %copy-start = (bf16[304,128]{1,0:T(8,128)(2,1)S(1)}, bf16[304,128]{1,0:T(8,128)(2,1)}, u32[]{:S(2)}) copy-start(bf16[304,128]{1,0:T(8,128)(2,1)} %left_ref.1) | copy-start | bytes 233476
